TPU v7x, 32 devices: a whole 2x2x4 slice. The times are simulated.
32 devices in a mesh: dp: 8 (over z, y), tensor: 4 (over x, core).
Axes of the slice: x: 2, y: 2, z: 4, core: 2. Of those that a mesh axis runs over, the one named last changes fastest.
Arguments:
- tokens: bfloat16 [16384, 768], P(('dp', 'tensor')), may hold values from -6 to 6
- grad_out: bfloat16 [16384, 768], P(('dp', 'tensor')), may hold values from -6 to 6
- seg_ids: int32 [16, 1024], P('dp'), may hold values from 0 to 5, never falling along the last dimension, each value on 1 to 800 neighbouring positions
- w_qkv: bfloat16 [3, 768, 768], P(None, 'dp', 'tensor'), may hold values from -0.21875 to 0.21875
- b_qv: bfloat16 [2, 768], P(None, ('tensor', 'dp')), may hold values from -3 to 3
- w_out: bfloat16 [768, 768], P('tensor', 'dp'), may hold values from -1.75 to 1.75
- w_up: bfloat16 [768, 3072], P('dp', 'tensor'), may hold values from -0.21875 to 0.21875
- b_up: bfloat16 [3072], P(('tensor', 'dp')), may hold values from -3 to 3
- w_down: bfloat16 [3072, 768], P('tensor', 'dp'), may hold values from -0.21875 to 0.21875
- b_out: float32 [768], P(('dp', 'tensor')), may hold values from -2 to 2
- b_down: float32 [768], P(('dp', 'tensor')), may hold values from -2 to 2
- g_one: float32 [768], P(('dp', 'tensor')), may hold values from 0.5 to 1.5
- s_one: float32 [768], P(('dp', 'tensor')), may hold values from -2 to 2
- g_two: float32 [768], P(('dp', 'tensor')), may hold values from 0.5 to 1.5
- s_two: float32 [768], P(('dp', 'tensor')), may hold values from -2 to 2
Outputs:
- layer_out: bfloat16 [16384, 768], P(('dp', 'tensor'))
- input_grad: bfloat16 [16384, 768], P(('dp', 'tensor'))
- grad_qkv: float32 [3, 768, 768], P(None, 'dp', 'tensor')
- grad_bias_qv: float32 [2, 768], P(None, ('tensor', 'dp'))
- grad_out_proj: float32 [768, 768], P('tensor', 'dp')
- grad_up: float32 [768, 3072], P('dp', 'tensor')
- grad_bias_up: float32 [3072], P(('tensor', 'dp'))
- grad_down: float32 [3072, 768], P('tensor', 'dp')
- grad_bias_out: float32 [768], P(('dp', 'tensor'))
- grad_bias_down: float32 [768], P(('dp', 'tensor'))
- grad_gain_one: float32 [768], P(('dp', 'tensor'))
- grad_shift_one: float32 [768], P(('dp', 'tensor'))
- grad_gain_two: float32 [768], P(('dp', 'tensor'))
- grad_shift_two: float32 [768], P(('dp', 'tensor'))
Inputs may be any that keep to these rules, and one draw needn't show every extreme that they name: `seg_ids`: within a sequence the ids never fall; each document spans 1 to 800 tokens, and the longest one of a draw spans exactly 800.
All inputs are finite; a program needn't handle non-finite values.
Results may differ from a plain program's by a relative error of at most 0.024.
Values may be sent and summed in bfloat16 or wider, within the bound.
No kernel may reach another device: no remote copies, remote signals or barrier semaphores. Data moves between devices by JAX's collectives and lax.ppermute only.
A program may use at most 128 MiB of HBM per device.

v0:
```python
import jax
import jax.numpy as jnp
from jax import lax
from jax.sharding import PartitionSpec as P

HD = 64


EPSILON = 1e-05
ROOT_HALF = 0.7071067811865476


def norm_rows(r, gain, shift):
    mean = jnp.mean(r, axis=-1, keepdims=True)
    cent = r - mean
    var = jnp.mean(cent * cent, axis=-1, keepdims=True)
    return cent * lax.rsqrt(var + EPSILON) * gain + shift


def gelu_exact(u):
    return 0.5 * u * (1.0 + lax.erf(u * ROOT_HALF))


def masked_scores(query, keys, seg_query, seg_keys):
    raw = jnp.einsum("qhd,khd->hqk", query, keys, preferred_element_type=jnp.float32)
    same = seg_query[:, None] == seg_keys[None, :]
    return jnp.where(same[None], raw * 0.125, -1000000000.0)


def attend_forward(query, keys, values, seg_query, seg_keys):
    scores = masked_scores(query, keys, seg_query, seg_keys)
    top = jnp.max(scores, axis=-1, keepdims=True)
    expo = jnp.exp(scores - top)
    total = jnp.sum(expo, axis=-1, keepdims=True)
    probs = (expo / total).astype(jnp.bfloat16)
    context = jnp.einsum("hqk,khd->qhd", probs, values, preferred_element_type=jnp.float32)
    return (context.astype(jnp.bfloat16), top + jnp.log(total))


def attend_backward(query, keys, values, seg_query, seg_keys, lse_block, d_block):
    scores = masked_scores(query, keys, seg_query, seg_keys)
    probs = jnp.exp(scores - lse_block)
    probs_low = probs.astype(jnp.bfloat16)
    d_probs = jnp.einsum("qhd,khd->hqk", d_block, values, preferred_element_type=jnp.float32)
    inner = jnp.sum(probs * d_probs, axis=-1, keepdims=True)
    d_scores = (probs * (d_probs - inner)).astype(jnp.bfloat16)
    d_query = jnp.einsum("hqk,khd->qhd", d_scores, keys, preferred_element_type=jnp.float32) * 0.125
    d_keys = jnp.einsum("hqk,qhd->khd", d_scores, query, preferred_element_type=jnp.float32) * 0.125
    d_values = jnp.einsum("hqk,qhd->khd", probs_low, d_block, preferred_element_type=jnp.float32)
    return (d_query, d_keys, d_values)


def contract_rows(left, right):
    return lax.dot_general(
        left, right, (((0,), (0,)), ((), ())), preferred_element_type=jnp.float32
    )


def contract_cols(left, right):
    return lax.dot_general(
        left, right, (((1,), (1,)), ((), ())), preferred_element_type=jnp.float32
    )


def local(
    tokens,
    grad_out,
    seg_ids,
    w_qkv,
    b_qv,
    w_out,
    w_up,
    b_up,
    w_down,
    b_out,
    b_down,
    g_one,
    s_one,
    g_two,
    s_two,
):
    seqs, seq_len = seg_ids.shape
    group = seqs * seq_len
    block = min(512, seq_len)
    nblocks = seq_len // block
    items = seqs * nblocks
    wqkv_l, bqv_l, wout_l, wup_l, bup_l, wdown_l = (
        lax.all_gather(w_qkv, "dp", axis=1, tiled=True),
        lax.all_gather(b_qv, "dp", axis=1, tiled=True),
        lax.all_gather(w_out, "dp", axis=1, tiled=True),
        lax.all_gather(w_up, "dp", axis=0, tiled=True),
        lax.all_gather(b_up, "dp", axis=0, tiled=True),
        lax.all_gather(w_down, "dp", axis=1, tiled=True),
    )
    bout_f, bdown_f, gone_f, sone_f, gtwo_f, stwo_f = (
        lax.all_gather(b_out, ("dp", "tensor"), axis=0, tiled=True),
        lax.all_gather(b_down, ("dp", "tensor"), axis=0, tiled=True),
        lax.all_gather(g_one, ("dp", "tensor"), axis=0, tiled=True),
        lax.all_gather(s_one, ("dp", "tensor"), axis=0, tiled=True),
        lax.all_gather(g_two, ("dp", "tensor"), axis=0, tiled=True),
        lax.all_gather(s_two, ("dp", "tensor"), axis=0, tiled=True),
    )
    local_width = wqkv_l.shape[2]
    local_heads = local_width // HD
    x_full = lax.all_gather(tokens, "tensor", axis=0, tiled=True)
    proj = jnp.einsum("td,jde->jte", x_full, wqkv_l, preferred_element_type=jnp.float32)
    biases = jnp.stack([bqv_l[0], jnp.zeros_like(bqv_l[0]), bqv_l[1]]).astype(jnp.float32)
    proj = (proj + biases[:, None, :]).astype(jnp.bfloat16)
    heads = proj.reshape(3, seqs, seq_len, local_heads, HD)
    queries = heads[0].reshape(items, block, local_heads, HD)
    seg_blocks = seg_ids.reshape(items, block)
    owner = jnp.arange(items, dtype=jnp.int32) // nblocks

    def forward_item(item):
        query, seg_query, which = item
        return attend_forward(query, heads[1][which], heads[2][which], seg_query, seg_ids[which])

    context, lse = lax.map(forward_item, (queries, seg_blocks, owner))
    context = context.reshape(group, local_width)
    part = context
    attn = (
        lax.psum_scatter(
            jnp.dot(part, wout_l, preferred_element_type=jnp.float32).astype(jnp.bfloat16),
            "tensor",
            scatter_dimension=0,
            tiled=True,
        ).astype(jnp.float32)
        + bout_f
    )
    first = tokens.astype(jnp.float32) + attn
    normed = norm_rows(first, gone_f, sone_f)
    normed_full = lax.all_gather(normed.astype(jnp.bfloat16), "tensor", axis=0, tiled=True)
    up = jnp.dot(normed_full, wup_l, preferred_element_type=jnp.float32) + bup_l.astype(jnp.float32)
    hidden = gelu_exact(up).astype(jnp.bfloat16)
    part = hidden
    branch = (
        lax.psum_scatter(
            jnp.dot(part, wdown_l, preferred_element_type=jnp.float32).astype(jnp.bfloat16),
            "tensor",
            scatter_dimension=0,
            tiled=True,
        ).astype(jnp.float32)
        + bdown_f
    )
    second = normed + branch
    layer_out = norm_rows(second, gtwo_f, stwo_f)
    wqkv_b, wout_b, wup_b, wdown_b = (
        lax.all_gather(w_qkv, "dp", axis=1, tiled=True),
        lax.all_gather(w_out, "dp", axis=1, tiled=True),
        lax.all_gather(w_up, "dp", axis=0, tiled=True),
        lax.all_gather(w_down, "dp", axis=1, tiled=True),
    )
    _, pull_two = jax.vjp(norm_rows, second, gtwo_f, stwo_f)
    d_second, d_gain_two, d_shift_two = pull_two(grad_out.astype(jnp.float32))
    d_branch = d_second.astype(jnp.bfloat16)
    d_bias_down = jnp.sum(d_branch.astype(jnp.float32), axis=0)
    branch_full = lax.all_gather(d_branch, "tensor", axis=0, tiled=True)
    grad_down_w = contract_rows(hidden, branch_full)
    d_hidden = contract_cols(branch_full, wdown_b)
    _, pull_gelu = jax.vjp(gelu_exact, up)
    d_up = pull_gelu(d_hidden)[0].astype(jnp.bfloat16)
    grad_bias_up = jnp.sum(d_up.astype(jnp.float32), axis=0)
    grad_up_w = contract_rows(normed_full, d_up)
    part = d_up
    d_normed = d_second + lax.psum_scatter(
        contract_cols(part, wup_b).astype(jnp.bfloat16), "tensor", scatter_dimension=0, tiled=True
    ).astype(jnp.float32)
    _, pull_one = jax.vjp(norm_rows, first, gone_f, sone_f)
    d_first, d_gain_one, d_shift_one = pull_one(d_normed)
    d_attn = d_first.astype(jnp.bfloat16)
    d_bias_out = jnp.sum(d_attn.astype(jnp.float32), axis=0)
    attn_full = lax.all_gather(d_attn, "tensor", axis=0, tiled=True)
    grad_out_w = contract_rows(context, attn_full)
    d_context = contract_cols(attn_full, wout_b).astype(jnp.bfloat16)
    d_ctx_blocks = d_context.reshape(items, block, local_heads, HD)

    def backward_item(item):
        query, seg_query, which, lse_block, d_block = item
        return attend_backward(
            query, heads[1][which], heads[2][which], seg_query, seg_ids[which], lse_block, d_block
        )

    d_query, d_keys, d_values = lax.map(
        backward_item, (queries, seg_blocks, owner, lse, d_ctx_blocks)
    )
    d_keys = jnp.sum(d_keys.reshape(seqs, nblocks, seq_len, local_heads, HD), axis=1)
    d_values = jnp.sum(d_values.reshape(seqs, nblocks, seq_len, local_heads, HD), axis=1)
    d_proj = jnp.stack(
        [
            d_query.reshape(group, local_width),
            d_keys.reshape(group, local_width),
            d_values.reshape(group, local_width),
        ]
    ).astype(jnp.bfloat16)
    proj_sums = jnp.sum(d_proj.astype(jnp.float32), axis=1)
    grad_bias_qv = jnp.stack([proj_sums[0], proj_sums[2]])
    grad_qkv_w = jnp.einsum("td,jte->jde", x_full, d_proj, preferred_element_type=jnp.float32)
    part = d_proj
    d_tokens = d_first + lax.psum_scatter(
        jnp.einsum("jte,jde->td", part, wqkv_b, preferred_element_type=jnp.float32).astype(
            jnp.bfloat16
        ),
        "tensor",
        scatter_dimension=0,
        tiled=True,
    ).astype(jnp.float32)
    g_qkv, g_bqv, g_out, g_up, g_bup, g_down = (
        lax.psum_scatter(grad_qkv_w, "dp", scatter_dimension=1, tiled=True),
        lax.psum_scatter(grad_bias_qv, "dp", scatter_dimension=1, tiled=True),
        lax.psum_scatter(grad_out_w, "dp", scatter_dimension=1, tiled=True),
        lax.psum_scatter(grad_up_w, "dp", scatter_dimension=0, tiled=True),
        lax.psum_scatter(grad_bias_up, "dp", scatter_dimension=0, tiled=True),
        lax.psum_scatter(grad_down_w, "dp", scatter_dimension=1, tiled=True),
    )
    g_bout, g_bdown, g_gone, g_sone, g_gtwo, g_stwo = (
        lax.psum_scatter(d_bias_out, ("dp", "tensor"), scatter_dimension=0, tiled=True),
        lax.psum_scatter(d_bias_down, ("dp", "tensor"), scatter_dimension=0, tiled=True),
        lax.psum_scatter(d_gain_one, ("dp", "tensor"), scatter_dimension=0, tiled=True),
        lax.psum_scatter(d_shift_one, ("dp", "tensor"), scatter_dimension=0, tiled=True),
        lax.psum_scatter(d_gain_two, ("dp", "tensor"), scatter_dimension=0, tiled=True),
        lax.psum_scatter(d_shift_two, ("dp", "tensor"), scatter_dimension=0, tiled=True),
    )
    return (
        layer_out.astype(jnp.bfloat16),
        d_tokens.astype(jnp.bfloat16),
        g_qkv,
        g_bqv,
        g_out,
        g_up,
        g_bup,
        g_down,
        g_bout,
        g_bdown,
        g_gone,
        g_sone,
        g_gtwo,
        g_stwo,
    )


def solution(mesh):
    return jax.shard_map(
        local,
        mesh=mesh,
        in_specs=(
            P(("dp", "tensor"), None),
            P(("dp", "tensor"), None),
            P("dp", None),
            P(None, "dp", "tensor"),
            P(None, ("tensor", "dp")),
            P("tensor", "dp"),
            P("dp", "tensor"),
            P(("tensor", "dp")),
            P("tensor", "dp"),
            P(("dp", "tensor")),
            P(("dp", "tensor")),
            P(("dp", "tensor")),
            P(("dp", "tensor")),
            P(("dp", "tensor")),
            P(("dp", "tensor")),
        ),
        out_specs=(
            P(("dp", "tensor"), None),
            P(("dp", "tensor"), None),
            P(None, "dp", "tensor"),
            P(None, ("tensor", "dp")),
            P("tensor", "dp"),
            P("dp", "tensor"),
            P(("tensor", "dp")),
            P("tensor", "dp"),
            P(("dp", "tensor")),
            P(("dp", "tensor")),
            P(("dp", "tensor")),
            P(("dp", "tensor")),
            P(("dp", "tensor")),
            P(("dp", "tensor")),
        ),
        check_vma=False,
    )
```

profile of v0, /device:TPU:0, one launch (start us, length us, event | category | flops | bytes accessed | tf_op | source)
XLA Modules:
  0.0 854.5 jit_solution(17377182914923498748)
XLA Ops:
  8.8 22.3 %all-gather = bf16[8,24,2]{1,2,0:T(2,128)(2,1)S(1)} all-gather(bf16[1,24,2]{1,2,0:T(2,128)(2,1)} %bitcast.205), channel_id=1, replica_groups=mesh['dp'=8,'tensor'=4] {'dp'}, dimensions={0}, use_global_device_ids=true | all-gather | bytes 864 | tf_op jit(solution)/shard_map/all_gather | solution.py:89
  34.5 31.1 %all_gather.55 = bf16[192,768]{0,1:T(8,128)(2,1)S(1)} all-gather(bf16[192,96]{0,1:T(8,128)(2,1)S(1)} %copy.55), channel_id=1, replica_groups=mesh['dp'=8,'tensor'=4] {'dp'}, dimensions={1}, use_global_device_ids=true | all-gather | bytes 331776 | tf_op jit(solution)/shard_map/all_gather | solution.py:90
  65.6 35.3 %all_gather.52 = bf16[3,768,192]{2,0,1:T(4,128)(2,1)} all-gather(bf16[3,96,192]{2,0,1:T(4,128)(2,1)S(1)} %copy.49), channel_id=1, replica_groups=mesh['dp'=8,'tensor'=4] {'dp'}, dimensions={1}, use_global_device_ids=true | all-gather | bytes 995328 | tf_op jit(solution)/shard_map/all_gather | solution.py:88
  100.9 5.2 fusion.60
  114.2 40.8 %while.26 = (s32[]{:T(128)}, bf16[4,512,3,64]{1,3,2,0:T(8,128)(2,1)}, f32[4,3,512,1]{2,1,3,0:T(4,128)}, bf16[3,2,1024,3,64]{2,4,3,1,0:T(8,128)(2,1)S(1)}, s32[4]...) while((s32[]{:T(128)}, ...), condition=%wide.region_3.4_spmd, body=%wide.region_0.3_spmd.sunk | while | flops 422148608 | bytes 25370816 | solution.py:118
  168.5 39.5 %all-reduce.16 = (f32[768]{0:T(1024)}, f32[768]{0:T(1024)}, f32[768]{0:T(1024)S(1)}, f32[768]{0:T(1024)}, f32[768]{0:T(1024)}) all-reduce(f32[768]{0:T(1024)} %dynamic-update-slice.2, f32[768]{0:T(1024)} %dynamic-update-slice.1, f32[768]{0:T(1024)} %dynamic-update-slice, ...), channel_id=1, replica_groups=mesh['dp'=8,'tensor'=4] {'dp','tensor'}, use_global_device_ids=true, to_apply=%add.2 | all-reduce | flops 3840 | bytes 30720
  218.3 21.6 %all-reduce.3 = bf16[768]{0:T(1024)(128)(2,1)} all-reduce(bf16[768]{0:T(1024)(128)(2,1)} %dynamic-update-slice.3), channel_id=1, replica_groups=mesh['dp'=8,'tensor'=4] {'dp'}, use_global_device_ids=true, to_apply=%add.3 | all-reduce | flops 768 | bytes 3072
  243.2 7.0 multiply_convert_fusion.1
  250.1 36.9 %all-gather.14.cloned.1.call-done = bf16[768,768]{0,1:T(8,128)(2,1)} async-done(((bf16[768,96]{0,1:T(8,128)(2,1)}), bf16[768,768]{0,1:T(8,128)(2,1)}) %all-gather.14.cloned.1.call-update) | async-done | bytes 1179664 | tf_op jit(solution)/shard_map/all_gather | solution.py:93
  287.0 6.5 convolution_convert_fusion.1
  293.6 36.3 %reduce-scatter.16.cloned.1.call-done = bf16[512,768]{1,0:T(8,128)(2,1)} async-done(((bf16[2048,768]{1,0:T(8,128)(2,1)}), bf16[512,768]{1,0:T(8,128)(2,1)}) %reduce-scatter.16.cloned.1.call-update) | async-done | bytes 786448 | tf_op jit(solution)/shard_map/reduce_scatter | solution.py:137
  337.4 28.6 %all-gather.16.cloned.1.call-done = bf16[2048,768]{1,0:T(8,128)(2,1)} async-done(((bf16[512,768]{1,0:T(8,128)(2,1)}), bf16[2048,768]{1,0:T(8,128)(2,1)}) %all-gather.16.cloned.1.call-update) | async-done | bytes 3145744 | tf_op jit(solution)/shard_map/all_gather | solution.py:157
  366.0 8.0 convert_reduce_fusion
  375.7 4.0 convolution_convert_fusion
  379.8 37.9 %reduce-scatter.18.cloned.1.call-done = bf16[512,768]{1,0:T(8,128)(2,1)} async-done(((bf16[2048,768]{1,0:T(8,128)(2,1)}), bf16[512,768]{1,0:T(8,128)(2,1)}) %reduce-scatter.18.cloned.1.call-update) | async-done | bytes 786448 | tf_op jit(solution)/shard_map/reduce_scatter | solution.py:165
  426.3 28.4 %all-gather.18.cloned.1.call-done = bf16[2048,768]{1,0:T(8,128)(2,1)} async-done(((bf16[512,768]{1,0:T(8,128)(2,1)}), bf16[2048,768]{1,0:T(8,128)(2,1)}) %all-gather.18.cloned.1.call-update) | async-done | bytes 3145744 | tf_op jit(solution)/shard_map/all_gather | solution.py:172
  454.8 4.0 convolution_convert_fusion.3
  463.9 61.6 %while.27 = (s32[]{:T(128)}, bf16[4,512,3,64]{1,3,2,0:T(8,128)(2,1)}, f32[4,1024,3,64]{1,3,2,0:T(8,128)}, f32[4,1024,3,64]{1,3,2,0:T(8,128)}, bf16[3,2,1024,3,64...) while((s32[]{:T(128)}, ...), condition=%wide.region_17.18_spmd, body=%wide.region_15.17_spmd.sunk | while | flops 1031043584 | bytes 65866036 | solution.py:183
  525.6 4.4 convolution_bitcast_fusion
  531.5 4.6 bitcast_reduce_fusion
  547.7 6.0 fusion.67
  553.7 4.2 copy.64
  557.9 4.7 reshape.255
  562.7 5.6 bitcast_convert_fusion
  568.6 7.0 fusion.86
  575.7 6.9 fusion.87
  584.4 40.5 %all-reduce.15 = (f32[768]{0:T(1024)S(1)}, f32[768]{0:T(1024)S(1)}, f32[768]{0:T(1024)S(1)}, f32[768]{0:T(1024)S(1)}, f32[768]{0:T(1024)S(1)}, /*index=5*/f32[768]{0:T(1024)S(1)}, f32[768]{0:T(1024)S(1)}) all-reduce(f32[768]{0:T(1024)S(1)} %dynamic-update-slice.6, ...), channel_id=1, replica_groups=mesh['dp'=8,'tensor'=4] {'dp','tensor'}, use_global_device_ids=true, to_apply=%add.6 | all-reduce | flops 5376 | bytes 43008
  630.0 21.5 %all-reduce.17 = (f32[2,192]{1,0:T(2,128)S(1)}, f32[768]{0:T(1024)S(1)}) all-reduce(f32[2,192]{1,0:T(2,128)S(1)} %pad_maximum_fusion, f32[768]{0:T(1024)S(1)} %copy-done.40), channel_id=7, replica_groups=mesh['dp'=8,'tensor'=4] {'dp'}, use_global_device_ids=true, to_apply=%region_23.24.clone | all-reduce | flops 1152 | bytes 9216
  654.3 8.0 reduce-scatter.26.cloned.1.call-done
  664.2 37.5 %reduce-scatter.20.cloned.1.call-done = bf16[512,768]{1,0:T(8,128)(2,1)} async-done(((bf16[2048,768]{1,0:T(8,128)(2,1)}), bf16[512,768]{1,0:T(8,128)(2,1)}) %reduce-scatter.20.cloned.1.call-update) | async-done | bytes 786448 | tf_op jit(solution)/shard_map/reduce_scatter | solution.py:199
  704.0 70.6 %reduce-scatter.22.cloned.1.call-done = f32[96,768]{1,0:T(8,128)} async-done(((f32[768,768]{1,0:T(8,128)}), f32[96,768]{1,0:T(8,128)}) %reduce-scatter.22.cloned.1.call-update) | async-done | bytes 294928 | tf_op jit(solution)/shard_map/reduce_scatter | solution.py:211
  774.6 72.4 %reduce-scatter.24.cloned.1.call-done = f32[768,96]{0,1:T(8,128)} async-done(((f32[768,768]{0,1:T(8,128)}), f32[768,96]{0,1:T(8,128)}) %reduce-scatter.24.cloned.1.call-update) | async-done | bytes 294928 | tf_op jit(solution)/shard_map/reduce_scatter | solution.py:213
  (311 shorter events, 173.7 us)
Async XLA Ops:
  8.0 92.9 %all-gather.8.cloned.1.call-start = ((), (), s32[]{:S(2)}) async-start(), calls=%async_computation.8 | async-start | bytes 3932160 | tf_op jit(solution)/shard_map/all_gather | solution.py:105
  8.7 199.3 %reduce-scatter.14.cloned.1.call-start = ((), (), s32[]{:S(2)}) async-start(), calls=%async_computation.9 | async-start | bytes 3932160 | tf_op jit(solution)/shard_map/reduce_scatter | solution.py:122
  155.1 5.8 copy-start.21
  160.9 47.1 %copy-start.2 = (bf16[512,768]{1,0:T(8,128)(2,1)S(1)}, bf16[512,768]{1,0:T(8,128)(2,1)}, u32[]{:S(2)}) copy-start(bf16[512,768]{1,0:T(8,128)(2,1)} %param.19) | copy-start | bytes 2359300
  160.9 80.3 %all-gather.12.cloned.1.call-start = ((), (), s32[]{:S(2)}) async-start(), calls=%async_computation.11 | async-start | bytes 1327104 | tf_op jit(solution)/shard_map/all_gather | solution.py:91
  161.5 81.7 %all-gather.10.cloned.1.call-start = ((), (), s32[]{:S(2)}) async-start(), calls=%async_computation.10 | async-start | bytes 3932160 | tf_op jit(solution)/shard_map/all_gather | solution.py:132
  162.6 4.5 copy-start.36
  208.0 4.3 copy-start.3
  208.0 4.3 copy-start.22
  208.0 4.3 copy-start.37
  213.7 73.3 %all-gather.14.cloned.1.call-start = ((), (), s32[]{:S(2)}) async-start(), calls=%async_computation.12 | async-start | bytes 1327104 | tf_op jit(solution)/shard_map/all_gather | solution.py:93
  214.3 115.7 %reduce-scatter.16.cloned.1.call-start = ((), (), s32[]{:S(2)}) async-start(), calls=%async_computation.13 | async-start | bytes 3932160 | tf_op jit(solution)/shard_map/reduce_scatter | solution.py:137
  293.5 72.5 %all-gather.16.cloned.1.call-start = ((), (), s32[]{:S(2)}) async-start(), calls=%async_computation.14 | async-start | bytes 3932160 | tf_op jit(solution)/shard_map/all_gather | solution.py:157
  337.3 80.4 %reduce-scatter.18.cloned.1.call-start = ((), (), s32[]{:S(2)}) async-start(), calls=%async_computation.15 | async-start | bytes 3932160 | tf_op jit(solution)/shard_map/reduce_scatter | solution.py:165
  366.0 9.7 %copy-start.41 = (bf16[768,768]{1,0:T(8,128)(2,1)S(1)}, bf16[768,768]{1,0:T(8,128)(2,1)}, u32[]{:S(2)}) copy-start(bf16[768,768]{1,0:T(8,128)(2,1)} %all-gather.12.cloned.1.call-done) | copy-start | bytes 3538948
  379.7 75.0 %all-gather.18.cloned.1.call-start = ((), (), s32[]{:S(2)}) async-start(), calls=%async_computation.16 | async-start | bytes 3932160 | tf_op jit(solution)/shard_map/all_gather | solution.py:172
  417.7 4.3 copy-start.23
  426.1 226.6 %reduce-scatter.28.cloned.1.call-start = ((), (), s32[]{:S(2)}) async-start(), calls=%async_computation.21 | async-start | bytes 884736
  458.7 5.2 copy-start.8
  458.7 5.2 copy-start.44
  525.6 4.7 copy-start.19
  530.0 132.3 %reduce-scatter.26.cloned.1.call-start = ((), (), s32[]{:S(2)}) async-start(), calls=%async_computation.20 | async-start | bytes 2211840
  547.7 15.0 %copy-start.11 = (bf16[3,2048,192]{1,2,0:T(8,128)(2,1)}, bf16[3,2048,192]{1,2,0:T(8,128)(2,1)S(1)}, u32[]{:S(2)}) copy-start(bf16[3,2048,192]{1,2,0:T(8,128)(2,1)S(1)} %constant_dynamic-update-slice_fusion) | copy-start | bytes 7077892
  562.7 139.1 %reduce-scatter.20.cloned.1.call-start = ((), (), s32[]{:S(2)}) async-start(), calls=%async_computation.17 | async-start | bytes 3932160 | tf_op jit(solution)/shard_map/reduce_scatter | solution.py:199
  568.3 206.3 %reduce-scatter.22.cloned.1.call-start = ((), (), s32[]{:S(2)}) async-start(), calls=%async_computation.18 | async-start | bytes 2654208 | tf_op jit(solution)/shard_map/reduce_scatter | solution.py:211
  575.6 271.4 %reduce-scatter.24.cloned.1.call-start = ((), (), s32[]{:S(2)}) async-start(), calls=%async_computation.19 | async-start | bytes 2654208 | tf_op jit(solution)/shard_map/reduce_scatter | solution.py:213
  582.6 45.8 %copy-start.1 = (f32[512,768]{1,0:T(8,128)S(1)}, f32[512,768]{1,0:T(8,128)}, u32[]{:S(2)}) copy-start(f32[512,768]{1,0:T(8,128)} %copy-done) | copy-start | bytes 4718596
  582.6 45.7 %copy-start.26 = (f32[512]{0:T(512)S(1)}, f32[512]{0:T(512)}, u32[]{:S(2)}) copy-start(f32[512]{0:T(512)} %copy-done.25) | copy-start | bytes 6148
  582.6 45.7 %copy-start.28 = (f32[768]{0:T(1024)S(1)}, f32[768]{0:T(1024)}, u32[]{:S(2)}) copy-start(f32[768]{0:T(1024)} %get-tuple-element.275) | copy-start | bytes 9220
  582.7 45.7 %copy-start.31 = (f32[512]{0:T(512)S(1)}, f32[512]{0:T(512)}, u32[]{:S(2)}) copy-start(f32[512]{0:T(512)} %copy-done.30) | copy-start | bytes 6148
  624.9 4.7 copy-start.12
  629.6 72.1 %copy-start.10 = (f32[512,768]{1,0:T(8,128)S(1)}, f32[512,768]{1,0:T(8,128)}, u32[]{:S(2)}) copy-start(f32[512,768]{1,0:T(8,128)} %copy-done.9) | copy-start | bytes 4718596
  (37 other events, 69.4 us)
Sparse Core Ops, SparseCore 0:
  10.4 31.2 all-gather.7
  161.0 36.9 reduce-scatter.13
  337.5 28.5 all-gather.15
  426.2 28.5 all-gather.17
Sparse Core Ops, SparseCore 1:
  163.6 40.2 all-gather.11
  213.8 29.3 all-gather.9
  245.4 41.5 all-gather.13
  293.6 36.3 reduce-scatter.15
  379.8 37.8 reduce-scatter.17
  530.1 62.5 reduce-scatter.27
  596.0 66.3 reduce-scatter.25
  664.9 36.8 reduce-scatter.19
  705.7 68.9 reduce-scatter.21
  778.7 68.2 reduce-scatter.23
where the time goes:
time: 865 us; the launch traced here: 855 us
  waiting for transfers between devices  361 us (42%)
  blocking collectives  212 us (25%)
  matrix products  120 us (14%)
  local copies, waits for them, and re-layouts  79.5 us (9%)
  other arithmetic  47.5 us (5%)
  between operations  18.4 us (2%)
  loops' own time  16 us (2%)
    unnamed x4, blocking collectives  123 us
    reduce_scatter x1, waiting for transfers between devices, local(): lax.psum_scatter(grad_down_w, 'dp', scatter_dimension=1, tiled=True)  72.4 us
    reduce_scatter x1, waiting for transfers between devices, local(): lax.psum_scatter(grad_up_w, 'dp', scatter_dimension=0, tiled=True)  70.6 us
    reduce_scatter x1, waiting for transfers between devices, local(): lax.psum_scatter(contract_cols(part, wup_b).astype(jnp.bfloat16), 'tensor...  37.9 us
    reduce_scatter x1, waiting for transfers between devices, local(): lax.psum_scatter(jnp.einsum('jte,jde->td', part, wqkv_b, preferred_elemen...  37.5 us
    unnamed x120, local copies, waits for them, and re-layouts  37.3 us
    all_gather x1, waiting for transfers between devices, local(): lax.all_gather(w_down, 'dp', axis=1, tiled=True)  36.9 us
    reduce_scatter x1, waiting for transfers between devices, local(): lax.psum_scatter(jnp.dot(part, wdown_l, preferred_element_type=jnp.float3...  36.3 us
  transfers between devices with their start and end apart: 14, of which 10 were waited for; matrix products, arithmetic and copies ran while one was open for 11% of the time, Pallas kernels for 0%

commit v1 on v0

v1 whole, which is shorter than its diff:
```python
import functools

import jax
import jax.numpy as jnp
from jax import lax
from jax.experimental import pallas as pl
from jax.experimental.pallas import tpu as pltpu
from jax.sharding import Mesh, PartitionSpec as P

HD = 64
LANES = 128
EPSILON = 1e-05
ROOT_HALF = 0.7071067811865476
INV_ROOT_TWO_PI = 0.3989422804014327
F32 = jnp.float32
BF16 = jnp.bfloat16


def dot(a, b, dims):
    return lax.dot_general(a, b, (dims, ((), ())), preferred_element_type=F32)


def dot_nn(a, b):
    return dot(a, b, ((1,), (0,)))


def dot_nt(a, b):
    return dot(a, b, ((1,), (1,)))


def dot_tn(a, b):
    return dot(a, b, ((0,), (0,)))


def attention_forward_kernel(width, seg_q_ref, seg_k_ref, q_ref, k_ref, v_ref, ctx_ref, lse_ref):
    lane = lax.broadcasted_iota(jnp.int32, (1, LANES), 1)
    bias = jnp.where(seg_q_ref[...] == seg_k_ref[...], 0.0, -1000000000.0)
    block = q_ref.shape[0]
    stats = jnp.zeros((block, LANES), F32)
    for pair in range(width // LANES):
        cols = slice(pair * LANES, (pair + 1) * LANES)
        q2 = q_ref[:, cols] * jnp.asarray(0.125, BF16)
        k2 = k_ref[:, cols]
        v2 = v_ref[:, cols]
        outs = []
        for half in range(2):
            mine = (lane // HD) == half
            qm = jnp.where(mine, q2, jnp.zeros_like(q2))
            s = dot_nt(qm, k2) + bias
            top = jnp.max(s, axis=-1, keepdims=True)
            e = jnp.exp(s - top)
            total = jnp.sum(e, axis=-1, keepdims=True)
            o = dot_nn(e.astype(BF16), v2) * (1.0 / total)
            outs.append(o)
            stats = jnp.where(lane == 2 * pair + half, top + jnp.log(total), stats)
        ctx_ref[:, cols] = jnp.where(lane < HD, outs[0], outs[1]).astype(BF16)
    lse_ref[...] = stats.T[: lse_ref.shape[0], :]


def attention_forward(qkv, seg_col, seg_row, block):
    rows, triple = qkv.shape
    width = triple // 3
    return pl.pallas_call(
        functools.partial(attention_forward_kernel, width),
        grid=(rows // block,),
        in_specs=[
            pl.BlockSpec((block, 1), lambda i: (i, 0)),
            pl.BlockSpec((1, rows), lambda i: (0, 0)),
            pl.BlockSpec((block, width), lambda i: (i, 0)),
            pl.BlockSpec((rows, width), lambda i: (0, 1)),
            pl.BlockSpec((rows, width), lambda i: (0, 2)),
        ],
        out_specs=[
            pl.BlockSpec((block, width), lambda i: (i, 0)),
            pl.BlockSpec((8, block), lambda i: (0, i)),
        ],
        out_shape=[
            jax.ShapeDtypeStruct((rows, width), BF16),
            jax.ShapeDtypeStruct((8, rows), F32),
        ],
        cost_estimate=pl.CostEstimate(
            flops=4 * rows * rows * width * 4,
            bytes_accessed=8 * rows * width,
            transcendentals=rows * rows * width // HD,
        ),
        name="attention_forward",
    )(seg_col, seg_row, qkv, qkv, qkv)


def attention_backward_kernel(
    width, seg_k_ref, seg_q_ref, q_ref, k_ref, v_ref, ctx_ref, lse_ref, d_ref, out_ref, dk_ref, dv_ref
):
    step = pl.program_id(0)
    block = q_ref.shape[0]
    lane = lax.broadcasted_iota(jnp.int32, (1, LANES), 1)

    @pl.when(step == 0)
    def _():
        dk_ref[...] = jnp.zeros_like(dk_ref)
        dv_ref[...] = jnp.zeros_like(dv_ref)

    bias = jnp.where(seg_k_ref[...] == seg_q_ref[...], 0.0, -1000000000.0)
    for pair in range(width // LANES):
        cols = slice(pair * LANES, (pair + 1) * LANES)
        q2 = q_ref[:, cols] * jnp.asarray(0.125, BF16)
        k2 = k_ref[:, cols]
        v2 = v_ref[:, cols]
        d2 = d_ref[:, cols]
        prod = (d2.astype(F32) * ctx_ref[:, cols].astype(F32)).T
        kt = (k2 * jnp.asarray(0.125, BF16)).T
        row = lax.broadcasted_iota(jnp.int32, (LANES, 1), 0)
        dq = None
        dk = None
        dv = None
        for half in range(2):
            mine = (lane // HD) == half
            qm = jnp.where(mine, q2, jnp.zeros_like(q2))
            dm = jnp.where(mine, d2, jnp.zeros_like(d2))
            ktm = jnp.where((row // HD) == half, kt, jnp.zeros_like(kt))
            inner = jnp.sum(prod[half * HD : (half + 1) * HD, :], axis=0, keepdims=True)
            head = 2 * pair + half
            lse = lse_ref[head : head + 1, :]
            p = jnp.exp(dot_nt(k2, qm) + bias - lse)
            dp = dot_nt(v2, dm)
            ds = (p * (dp - inner)).astype(BF16)
            dv_h = dot_nn(p.astype(BF16), dm)
            dk_h = dot_nn(ds, qm)
            dq_h = dot_nn(ktm, ds)
            dv = dv_h if dv is None else dv + dv_h
            dk = dk_h if dk is None else dk + dk_h
            dq = dq_h if dq is None else dq + dq_h
        dk_ref[:, cols] += dk
        dv_ref[:, cols] += dv
        out_ref[pl.ds(pl.multiple_of(step * block, block), block), cols] = dq.T.astype(BF16)

    @pl.when(step == pl.num_programs(0) - 1)
    def _():
        out_ref[:, width : 2 * width] = dk_ref[...].astype(BF16)
        out_ref[:, 2 * width : 3 * width] = dv_ref[...].astype(BF16)


def attention_backward(qkv, ctx, lse, d_ctx, seg_col, seg_row, block):
    rows, triple = qkv.shape
    width = triple // 3
    return pl.pallas_call(
        functools.partial(attention_backward_kernel, width),
        grid=(rows // block,),
        in_specs=[
            pl.BlockSpec((rows, 1), lambda i: (0, 0)),
            pl.BlockSpec((1, block), lambda i: (0, i)),
            pl.BlockSpec((block, width), lambda i: (i, 0)),
            pl.BlockSpec((rows, width), lambda i: (0, 1)),
            pl.BlockSpec((rows, width), lambda i: (0, 2)),
            pl.BlockSpec((block, width), lambda i: (i, 0)),
            pl.BlockSpec((8, block), lambda i: (0, i)),
            pl.BlockSpec((block, width), lambda i: (i, 0)),
        ],
        out_specs=pl.BlockSpec((rows, triple), lambda i: (0, 0)),
        out_shape=jax.ShapeDtypeStruct((rows, triple), BF16),
        scratch_shapes=[pltpu.VMEM((rows, width), F32), pltpu.VMEM((rows, width), F32)],
        cost_estimate=pl.CostEstimate(
            flops=10 * rows * rows * width * 4,
            bytes_accessed=16 * rows * width,
            transcendentals=rows * rows * width // HD,
        ),
        name="attention_backward",
    )(seg_col, seg_row, qkv, qkv, qkv, ctx, lse, d_ctx)


def normalize(r):
    mean = jnp.mean(r, axis=-1, keepdims=True)
    cent = r - mean
    var = jnp.mean(cent * cent, axis=-1, keepdims=True)
    inv = lax.rsqrt(var + EPSILON)
    return cent * inv, inv


def normalize_back(hat, inv, gain, d_out):
    d_hat = d_out * gain
    first = jnp.mean(d_hat, axis=-1, keepdims=True)
    second = jnp.mean(d_hat * hat, axis=-1, keepdims=True)
    return inv * (d_hat - first - hat * second)


def swap(a):
    return lax.ppermute(a, "c", [(0, 1), (1, 0)])


def pair_gather(a):
    return jnp.concatenate([a, swap(a)], axis=0)


def pair_sum(full, rows):
    return full[:rows] + swap(full[rows:].astype(BF16)).astype(F32)


def gather_units(a):
    ndp = lax.axis_size("dp")
    nx = lax.axis_size("x")
    g = lax.all_gather(a, ("dp", "x"), axis=0, tiled=False)
    g = g.reshape(ndp, nx, *a.shape)
    return jnp.transpose(g, (1, 0, 2, 3)).reshape(nx, ndp * a.shape[0], a.shape[1])


def scatter_units(g):
    ndp = lax.axis_size("dp")
    nx, model, cols = g.shape
    g = g.reshape(nx, ndp, model // ndp, cols)
    g = jnp.transpose(g, (1, 0, 2, 3)).reshape(ndp * nx * (model // ndp), cols)
    return lax.psum_scatter(g, ("dp", "x"), scatter_dimension=0, tiled=True)


def local(
    tokens, grad_out, seg_ids, w_qkv, b_qv, w_out, w_up, b_up, w_down, b_out, b_down, g_one, s_one, g_two, s_two
):
    ndp = lax.axis_size("dp")
    nx = lax.axis_size("x")
    parity = lax.axis_index("c")
    which = lax.axis_index("x")
    rows, model = tokens.shape
    piece = model // ndp
    part = w_qkv.shape[2]
    width = nx * part

    seg = lax.dynamic_index_in_dim(seg_ids, which, 0, keepdims=False)
    seg_two = seg.reshape(2, rows)
    seg_rel = jnp.concatenate(
        [
            lax.dynamic_index_in_dim(seg_two, parity, 0, keepdims=False),
            lax.dynamic_index_in_dim(seg_two, 1 - parity, 0, keepdims=False),
        ]
    )
    seg_col = seg_rel[:, None]
    seg_row = seg_rel[None, :]

    unit_a = jnp.concatenate([w_qkv[0], w_qkv[1], w_qkv[2], w_out.T], axis=1)
    a_full = gather_units(unit_a)
    b_full = gather_units(w_up)
    c_full = gather_units(w_down.T)
    slim = model // (ndp * nx * 2)
    small = jnp.concatenate(
        [
            b_out,
            b_down,
            g_one,
            s_one,
            g_two,
            s_two,
            b_qv.reshape(-1).astype(F32),
            b_up.astype(F32),
        ]
    )
    small = lax.all_gather(small, ("dp", "x", "c"), axis=0, tiled=False)
    vectors = jnp.transpose(small[:, : 6 * slim].reshape(ndp * nx * 2, 6, slim), (1, 0, 2)).reshape(6, model)
    bout_f, bdown_f, gone_f, sone_f, gtwo_f, stwo_f = [vectors[i : i + 1] for i in range(6)]
    wide = small[:, 6 * slim :].reshape(ndp, nx, 2, -1)
    wide = lax.dynamic_index_in_dim(wide, parity, 2, keepdims=False)
    qv = part // ndp
    bias_qv = jnp.transpose(wide[:, :, : 2 * qv].reshape(ndp, nx, 2, qv), (2, 1, 0, 3)).reshape(2, width)
    bias_qkv = jnp.concatenate([bias_qv[0], jnp.zeros((width,), F32), bias_qv[1]])[None]
    bias_up = jnp.transpose(wide[:, :, 2 * qv :], (1, 0, 2)).reshape(1, nx * model)

    x_own = tokens
    x_full = pair_gather(x_own)
    w_all = jnp.concatenate([a_full[i][:, j * part : (j + 1) * part] for j in range(3) for i in range(nx)], axis=1)
    o_t = jnp.concatenate([a_full[i][:, 3 * part :] for i in range(nx)], axis=1)
    b_all = jnp.concatenate([b_full[i] for i in range(nx)], axis=1)
    c_all = jnp.concatenate([c_full[i] for i in range(nx)], axis=1)

    qkv = (dot_nn(x_full, w_all) + bias_qkv).astype(BF16)
    block = 256
    ctx, lse = attention_forward(qkv, seg_col, seg_row, block)
    attn = pair_sum(dot_nt(ctx, o_t), rows)
    first = x_own.astype(F32) + attn + bout_f
    hat_one, inv_one = normalize(first)
    normed = hat_one * gone_f + sone_f
    normed_full = pair_gather(normed.astype(BF16))
    up = dot_nn(normed_full, b_all) + bias_up
    cdf = 0.5 * (1.0 + lax.erf(up * ROOT_HALF))
    hidden = (up * cdf).astype(BF16)
    slope = (cdf + up * (jnp.exp(-0.5 * up * up) * INV_ROOT_TWO_PI)).astype(BF16)
    branch = pair_sum(dot_nt(hidden, c_all), rows)
    second = normed + branch + bdown_f
    hat_two, inv_two = normalize(second)
    layer_out = (hat_two * gtwo_f + stwo_f).astype(BF16)

    g_in = grad_out.astype(F32)
    d_gain_two = jnp.sum(g_in * hat_two, axis=0)
    d_shift_two = jnp.sum(g_in, axis=0)
    d_second = normalize_back(hat_two, inv_two, gtwo_f, g_in)
    d_branch = d_second.astype(BF16)
    d_bias_down = jnp.sum(d_branch.astype(F32), axis=0)
    db_full = pair_gather(d_branch)
    grad_c = dot_tn(db_full, hidden).astype(BF16)
    d_hidden = dot_nn(db_full, c_all)
    d_up = (d_hidden * slope.astype(F32)).astype(BF16)
    d_bias_up = jnp.sum(d_up.astype(F32), axis=0)
    grad_b = dot_tn(normed_full, d_up).astype(BF16)
    d_normed = d_second + pair_sum(dot_nt(d_up, b_all), rows)
    d_gain_one = jnp.sum(d_normed * hat_one, axis=0)
    d_shift_one = jnp.sum(d_normed, axis=0)
    d_first = normalize_back(hat_one, inv_one, gone_f, d_normed)
    d_attn = d_first.astype(BF16)
    d_bias_out = jnp.sum(d_attn.astype(F32), axis=0)
    da_full = pair_gather(d_attn)
    grad_o = dot_tn(da_full, ctx).astype(BF16)
    d_ctx = dot_nn(da_full, o_t).astype(BF16)
    d_qkv = attention_backward(qkv, ctx, lse, d_ctx, seg_col, seg_row, block)
    d_bias_qkv = jnp.sum(d_qkv.astype(F32), axis=0)
    grad_w = dot_tn(x_full, d_qkv).astype(BF16)
    input_grad = (d_first + pair_sum(dot_nt(d_qkv, w_all), rows)).astype(BF16)

    unit_ga = jnp.stack(
        [
            jnp.concatenate(
                [grad_w[:, j * width + i * part : j * width + (i + 1) * part] for j in range(3)]
                + [grad_o[:, i * part : (i + 1) * part]],
                axis=1,
            )
            for i in range(nx)
        ]
    )
    ga = scatter_units(unit_ga).astype(F32)
    gb = scatter_units(jnp.stack([grad_b[:, i * model : (i + 1) * model] for i in range(nx)])).astype(F32)
    gc = scatter_units(jnp.stack([grad_c[:, i * model : (i + 1) * model] for i in range(nx)])).astype(F32)
    g_qkv = jnp.stack([ga[:, j * part : (j + 1) * part] for j in range(3)])
    g_out = ga[:, 3 * part :].T

    sums = jnp.stack([d_bias_out, d_bias_down, d_gain_one, d_shift_one, d_gain_two, d_shift_two])
    sums = jnp.transpose(sums.reshape(6, ndp * nx * 2, slim), (1, 0, 2)).reshape(ndp, nx, 2, 6 * slim)
    d_bqv = jnp.stack([d_bias_qkv[:width], d_bias_qkv[2 * width :]]).reshape(2, nx, ndp, qv)
    d_bqv = jnp.transpose(d_bqv, (2, 1, 0, 3)).reshape(ndp, nx, 1, 2 * qv)
    d_bup = jnp.transpose(d_bias_up.reshape(nx, ndp, piece), (1, 0, 2))[:, :, None]
    tail = jnp.concatenate([d_bqv, d_bup], axis=-1)
    tail = jnp.where(lax.broadcasted_iota(jnp.int32, (1, 1, 2, 1), 2) == parity, tail, 0.0)
    packed = jnp.concatenate([sums, tail], axis=-1).reshape(ndp * nx * 2, -1)
    mine = lax.psum_scatter(packed, ("dp", "x", "c"), scatter_dimension=0, tiled=True)[0]
    six = [mine[i * slim : (i + 1) * slim] for i in range(6)]
    g_bqv = mine[6 * slim : 6 * slim + 2 * qv].reshape(2, qv)
    g_bup = mine[6 * slim + 2 * qv :]
    return (layer_out, input_grad, g_qkv, g_bqv, g_out, gb, g_bup, gc.T, *six)


def solution(mesh):
    ndp, nt = mesh.devices.shape
    fine = Mesh(mesh.devices.reshape(ndp, nt // 2, 2), ("dp", "x", "c"))
    tensor = ("x", "c")
    every = ("dp", "x", "c")
    row = P(every, None)
    vec = P(every)
    return jax.shard_map(
        local,
        mesh=fine,
        in_specs=(
            row,
            row,
            P("dp", None),
            P(None, "dp", tensor),
            P(None, ("x", "c", "dp")),
            P(tensor, "dp"),
            P("dp", tensor),
            P(("x", "c", "dp")),
            P(tensor, "dp"),
            vec,
            vec,
            vec,
            vec,
            vec,
            vec,
        ),
        out_specs=(
            row,
            row,
            P(None, "dp", tensor),
            P(None, ("x", "c", "dp")),
            P(tensor, "dp"),
            P("dp", tensor),
            P(("x", "c", "dp")),
            P(tensor, "dp"),
            vec,
            vec,
            vec,
            vec,
            vec,
            vec,
        ),
        check_vma=False,
    )
```

time: 865 us -> 656 us (0.76)
  blocking collectives: 212 us -> 85.6 us
  matrix products: 120 us -> 49.1 us
  local copies, waits for them, and re-layouts: 79.5 us -> 42.7 us
  Pallas kernels: 0 us -> 35.8 us
  waiting for transfers between devices: 361 us -> 390 us
  other arithmetic: 47.5 us -> 25.7 us
  loops' own time: 16 us -> 0 us
    all_gather x3 -> x0, blocking collectives: 88.7 us -> none  [the longest x1 35.3 us: local(): lax.all_gather(w_qkv, 'dp', axis=1, tiled=True)]
    dot_general x39 -> x12, matrix products: 115 us -> 49.1 us  [dot(): return lax.dot_general(a, b, (dims, ((), ())), preferred_element_type=F32)]
    unnamed x4 -> x2, blocking collectives: 123 us -> 85.6 us
    pallas_call x0 -> x2, Pallas kernels: none -> 35.8 us  [the longest x1 20.6 us: attention_backward(): pl.pallas_call(functools.partial(attention_backward_kernel, width), grid=...]
    unnamed x120 -> x100, local copies, waits for them, and re-layouts: 37.3 us -> 11.2 us
    reduce_scatter x6 -> x3, waiting for transfers between devices: 255 us -> 279 us  [scatter_units(): return lax.psum_scatter(g, ('dp', 'x'), scatter_dimension=0, tiled=True)]
    another operation x2 -> x0, loops' own time: 16 us -> none  [the longest x1 8.04 us: local(): lax.map(backward_item, (queries, seg_blocks, owner, lse, d_ctx_blocks))]
    reduce_sum x16 -> x9, other arithmetic: 27.6 us -> 12.9 us  [the longest x1 4.55 us: local(): d_gain_one = jnp.sum(d_normed * hat_one, axis=0)]
  transfers between devices with their start and end apart: 14 -> 14, of which waited for: 10 -> 10; matrix products, arithmetic and copies ran while one was open for 11% -> 12% of each run, Pallas kernels for 0% -> 6%
where the time goes in v1:
time: 656 us; the launch traced here: 646 us
  waiting for transfers between devices  390 us (59%)
  blocking collectives  85.6 us (13%)
  matrix products  49.1 us (7%)
  local copies, waits for them, and re-layouts  42.7 us (7%)
  Pallas kernels  35.8 us (5%)
  other arithmetic  25.7 us (4%)
  between operations  15.5 us (2%)
    reduce_scatter x3, waiting for transfers between devices, scatter_units(): return lax.psum_scatter(g, ('dp', 'x'), scatter_dimension=0, tiled=True)  279 us
    all_gather x3, waiting for transfers between devices, gather_units(): g = lax.all_gather(a, ('dp', 'x'), axis=0, tiled=False)  104 us
    unnamed x2, blocking collectives  85.6 us
    dot_general x12, matrix products, dot(): return lax.dot_general(a, b, (dims, ((), ())), preferred_element_type=F32)  49.1 us
    pallas_call x1, Pallas kernels, attention_backward(): pl.pallas_call(functools.partial(attention_backward_kernel, width), grid=...  20.6 us
    pallas_call x1, Pallas kernels, attention_forward(): pl.pallas_call(functools.partial(attention_forward_kernel, width), grid=(...  15.2 us
  transfers between devices with their start and end apart: 14, of which 10 were waited for; matrix products, arithmetic and copies ran while one was open for 12% of the time, Pallas kernels for 6%

profile of v1, /device:TPU:0, one launch (start us, length us, event | category | flops | bytes accessed | tf_op | source)
XLA Modules:
  0.0 646.0 jit_solution(1499061907861578191)
XLA Ops:
  13.3 42.4 %all-reduce = f32[9216]{0:T(1024)S(1)} all-reduce(f32[9216]{0:T(1024)S(1)} %dynamic-update-slice), channel_id=3, replica_groups=mesh['dp'=8,'x'=2,'c'=2] {'dp','x','c'}, use_global_device_ids=true, to_apply=%add | all-reduce | flops 9216 | bytes 73728
  59.9 16.6 %all-gather.8.cloned.1.call-done = bf16[1536,768]{1,0:T(8,128)(2,1)} async-done(((bf16[96,768]{1,0:T(8,128)(2,1)}), bf16[1536,768]{1,0:T(8,128)(2,1)}) %all-gather.8.cloned.1.call-update) | async-done | bytes 2359312 | tf_op jit(solution)/shard_map/all_gather | solution.py:200
  76.5 1.8 fusion.43
  79.8 4.0 concatenate.59
  83.8 5.6 add_convert_fusion.q_ref.k_ref.v_ref
  89.3 15.2 %attention_forward.1 = (bf16[1024,384]{1,0:T(8,128)(2,1)}, f32[8,1024]{1,0:T(8,128)}) custom-call(s32[1024,1]{1,0:T(8,128)} %copy.125.seg_q_ref.seg_k_ref, s32[1,1024]{1,0:T(1,128)} %bitcast.130, bf16[1024,1152]{1,0:T(8,128)(2,1)} %add_convert_fusion.q_ref.k_ref.v_ref, bf16[1024,1152]{1,0:T(8,128)(2,1)} %add_convert_fusion.q_ref.k_ref.v_ref, ...), custom_call_target="tpu_custom_call" | custom-call | flops 6442450944 | bytes 3145728 | tf_op jit(solution)/shard_map/attention_forward/pallas_call | solution.py:63
  104.6 2.2 fusion.23
  110.9 1.9 fusion.38
  114.6 25.9 %all-gather.10.cloned.1.call-done = bf16[1536,768]{1,0:T(8,128)(2,1)} async-done(((bf16[96,768]{1,0:T(8,128)(2,1)}), bf16[1536,768]{1,0:T(8,128)(2,1)}) %all-gather.10.cloned.1.call-update) | async-done | bytes 2359312 | tf_op jit(solution)/shard_map/all_gather | solution.py:200
  140.5 2.8 fusion.44
  143.3 61.1 %all-gather.12.cloned.1.call-done = bf16[1536,768]{1,0:T(8,128)(2,1)} async-done(((bf16[96,768]{1,0:T(8,128)(2,1)}), bf16[1536,768]{1,0:T(8,128)(2,1)}) %all-gather.12.cloned.1.call-update) | async-done | bytes 2359312 | tf_op jit(solution)/shard_map/all_gather | solution.py:200
  204.4 1.9 fusion.42
  206.4 7.5 %multiply_convert_fusion.1 = (bf16[1024,1536]{1,0:T(8,128)(2,1)S(1)}, f32[1024,1536]{1,0:T(8,128)}) fusion(f32[1536]{0:T(1024)S(1)} %add.143, bf16[768,768]{1,0:T(8,128)(2,1)S(1)} %bitcast.115, bf16[768,768]{1,0:T(8,128)(2,1)S(1)} %bitcast.112, bf16[512,768]{1,0:T(8,128)(2,1)} %collective-permute-done.2, bf16[512,768]{1,0:T(8,128)(2,1)} %fusion.22), kind=kOutput, calls=%fused_computation.8 | convolution fusion | flops 2433220608 | bytes 13375488 | tf_op jit(solution)/shard_map/dot_general | solution.py:20
  214.0 2.6 fusion.19
  216.6 1.6 copy-done.7
  220.8 2.5 fusion.36
  227.3 2.1 collective-permute-done.4
  229.4 5.5 convert_reduce_fusion
  234.9 5.4 convolution_convert_fusion.1
  245.3 5.3 fusion.20
  253.2 2.9 convolution_convert_fusion
  258.1 4.6 multiply_reduce_fusion
  263.4 2.2 collective-permute-done.6
  265.5 2.0 convolution_convert_fusion.3.d_ref
  268.7 20.6 %attention_backward.1 = bf16[1024,1152]{1,0:T(8,128)(2,1)} custom-call(s32[1024,1]{1,0:T(8,128)} %copy.125.seg_q_ref.seg_k_ref, s32[1,1024]{1,0:T(1,128)} %bitcast.131, bf16[1024,1152]{1,0:T(8,128)(2,1)} %add_convert_fusion.q_ref.k_ref.v_ref, bf16[1024,1152]{1,0:T(8,128)(2,1)} %add_convert_fusion.q_ref.k_ref.v_ref, ...), custom_call_target="tpu_custom_call" | custom-call | flops 16106127360 | bytes 6291456 | tf_op jit(solution)/shard_map/attention_backward/pallas_call | solution.py:145
  289.3 4.4 convolution_convert_fusion.2
  298.4 4.6 fusion.53
  305.2 43.2 %all-reduce.1 = f32[32,288]{0,1:T(8,128)S(1)} all-reduce(f32[32,288]{0,1:T(8,128)S(1)} %pad_maximum_fusion.23), channel_id=7, replica_groups=mesh['dp'=8,'x'=2,'c'=2] {'dp','x','c'}, use_global_device_ids=true, to_apply=%region_17.18.clone | all-reduce | flops 9216 | bytes 73728
  350.7 2.7 fusion.13
  353.4 17.1 %reduce-scatter.7.cloned.1.call-done = bf16[96,768]{1,0:T(8,128)(2,1)} async-done(((bf16[1536,768]{1,0:T(8,128)(2,1)}), bf16[96,768]{1,0:T(8,128)(2,1)}) %reduce-scatter.7.cloned.1.call-update) | async-done | bytes 147472 | tf_op jit(solution)/shard_map/reduce_scatter | solution.py:210
  372.2 131.5 %reduce-scatter.9.cloned.1.call-done = bf16[96,768]{1,0:T(8,128)(2,1)} async-done(((bf16[1536,768]{1,0:T(8,128)(2,1)}), bf16[96,768]{1,0:T(8,128)(2,1)}) %reduce-scatter.9.cloned.1.call-update) | async-done | bytes 147472 | tf_op jit(solution)/shard_map/reduce_scatter | solution.py:210
  505.4 130.8 %reduce-scatter.5.cloned.1.call-done = bf16[96,768]{1,0:T(8,128)(2,1)} async-done(((bf16[1536,768]{1,0:T(8,128)(2,1)}), bf16[96,768]{1,0:T(8,128)(2,1)}) %reduce-scatter.5.cloned.1.call-update) | async-done | bytes 147472 | tf_op jit(solution)/shard_map/reduce_scatter | solution.py:210
  (230 shorter events, 50.0 us)
Async XLA Ops:
  7.2 49.6 %copy-start = (s32[2,1024]{1,0:T(2,128)S(1)}, s32[2,1024]{1,0:T(2,128)}, u32[]{:S(2)}) copy-start(s32[2,1024]{1,0:T(2,128)} %param.17) | copy-start | bytes 24580
  7.2 50.8 %copy-start.4 = (bf16[512,768]{1,0:T(8,128)(2,1)S(1)}, bf16[512,768]{1,0:T(8,128)(2,1)}, u32[]{:S(2)}) copy-start(bf16[512,768]{1,0:T(8,128)(2,1)} %param.15) | copy-start | bytes 2359300
  7.2 69.3 %all-gather.8.cloned.1.call-start = ((), (), s32[]{:S(2)}) async-start(), calls=%async_computation.6 | async-start | bytes 2506752 | tf_op jit(solution)/shard_map/all_gather | solution.py:200
  9.9 130.6 %all-gather.10.cloned.1.call-start = ((), (), s32[]{:S(2)}) async-start(), calls=%async_computation.7 | async-start | bytes 2506752 | tf_op jit(solution)/shard_map/all_gather | solution.py:200
  10.6 193.8 %all-gather.12.cloned.1.call-start = ((), (), s32[]{:S(2)}) async-start(), calls=%async_computation.8 | async-start | bytes 2506752 | tf_op jit(solution)/shard_map/all_gather | solution.py:200
  10.7 48.3 %collective-permute-start = (bf16[512,768]{1,0:T(8,128)(2,1)}, bf16[512,768]{1,0:T(8,128)(2,1)S(1)}, u32[]{:S(2)}, u32[]{:S(2)}) collective-permute-start(bf16[512,768]{1,0:T(8,128)(2,1)} %param.15), channel_id=1, source_target_pairs={{0,1},{1,0},{2,3},{3,2},{4,5},{5,4},{6,7},{7,6},{8,9},{9,8},{10,11... | collective-permute-start | bytes 2359304 | tf_op jit(solution)/shard_map/ppermute | solution.py:186
  11.4 359.2 %reduce-scatter.7.cloned.1.call-start = ((), (), s32[]{:S(2)}) async-start(), calls=%async_computation.4 | async-start | bytes 2506752 | tf_op jit(solution)/shard_map/reduce_scatter | solution.py:210
  79.8 24.8 %copy-start.9 = (bf16[768,192]{1,0:T(8,128)(2,1)}, bf16[768,192]{1,0:T(8,128)(2,1)S(1)}, u32[]{:S(2)}) copy-start(bf16[768,192]{1,0:T(8,128)(2,1)S(1)} %get-tuple-element.181) | copy-start | bytes 884740
  108.5 2.4 collective-permute-start.1
  114.3 92.1 %collective-permute-start.2 = (bf16[512,768]{1,0:T(8,128)(2,1)}, bf16[512,768]{1,0:T(8,128)(2,1)}, u32[]{:S(2)}, u32[]{:S(2)}) collective-permute-start(bf16[512,768]{1,0:T(8,128)(2,1)} %fusion.22), channel_id=1, source_target_pairs={{0,1},{1,0},{2,3},{3,2},{4,5},{5,4},{6,7},{7,6},{8,9},{9,8},{10,11... | collective-permute-start | bytes 2359304 | tf_op jit(solution)/shard_map/ppermute | solution.py:186
  114.6 91.8 %copy-start.37 = (f32[1536]{0:T(1024)}, f32[1536]{0:T(1024)S(1)}, u32[]{:S(2)}) copy-start(f32[1536]{0:T(1024)S(1)} %add.143) | copy-start | bytes 18436
  143.3 63.1 %copy-start.11 = (bf16[1,8,96,768]{3,2,0,1:T(8,128)(2,1)}, bf16[1,8,96,768]{3,2,0,1:T(8,128)(2,1)S(1)}, u32[]{:S(2)}) copy-start(bf16[1,8,96,768]{3,2,0,1:T(8,128)(2,1)S(1)} %get-tuple-element.134) | copy-start | bytes 3538948
  206.3 7.6 %copy-start.13 = (bf16[1,8,96,768]{3,2,0,1:T(8,128)(2,1)}, bf16[1,8,96,768]{3,2,0,1:T(8,128)(2,1)S(1)}, u32[]{:S(2)}) copy-start(bf16[1,8,96,768]{3,2,0,1:T(8,128)(2,1)S(1)} %get-tuple-element.130) | copy-start | bytes 3538948
  206.3 7.6 %copy-start.15 = (bf16[1,8,96,768]{3,2,0,1:T(8,128)(2,1)}, bf16[1,8,96,768]{3,2,0,1:T(8,128)(2,1)S(1)}, u32[]{:S(2)}) copy-start(bf16[1,8,96,768]{3,2,0,1:T(8,128)(2,1)S(1)} %get-tuple-element.131) | copy-start | bytes 3538948
  218.4 2.5 collective-permute-start.3
  220.8 8.6 %copy-start.44 = (f32[1024,1536]{1,0:T(8,128)S(1)}, f32[1024,1536]{1,0:T(8,128)}, u32[]{:S(2)}) copy-start(f32[1024,1536]{1,0:T(8,128)} %get-tuple-element.175) | copy-start | bytes 18874372
  225.9 3.5 copy-start.14
  225.9 3.5 copy-start.16
  225.9 3.5 copy-start.38
  227.1 7.9 %copy-start.18 = (bf16[512,768]{1,0:T(8,128)(2,1)}, bf16[512,768]{1,0:T(8,128)(2,1)S(1)}, u32[]{:S(2)}) copy-start(bf16[512,768]{1,0:T(8,128)(2,1)S(1)} %get-tuple-element.117) | copy-start | bytes 2359300
  227.1 2.4 collective-permute-start.4
  229.4 5.5 copy-start.39
  234.9 5.5 copy-start.43
  242.4 261.3 %reduce-scatter.9.cloned.1.call-start = ((), (), s32[]{:S(2)}) async-start(), calls=%async_computation.5 | async-start | bytes 2506752 | tf_op jit(solution)/shard_map/reduce_scatter | solution.py:210
  245.3 7.4 %copy-start.42 = (bf16[1024,1536]{1,0:T(8,128)(2,1)S(1)}, bf16[1024,1536]{1,0:T(8,128)(2,1)}, u32[]{:S(2)}) copy-start(bf16[1024,1536]{1,0:T(8,128)(2,1)} %copy-done.41) | copy-start | bytes 9437188
  252.5 5.5 collective-permute-start.5
  258.0 378.2 %reduce-scatter.5.cloned.1.call-start = ((), (), s32[]{:S(2)}) async-start(), calls=%async_computation.3 | async-start | bytes 2506752 | tf_op jit(solution)/shard_map/reduce_scatter | solution.py:210
  263.2 4.3 copy-start.17
  263.2 2.4 collective-permute-start.6
  298.4 4.9 copy-start.5
  303.0 47.7 %collective-permute-start.7 = (bf16[512,768]{1,0:T(8,128)(2,1)S(1)}, bf16[512,768]{1,0:T(8,128)(2,1)S(1)}, u32[]{:S(2)}, u32[]{:S(2)}) collective-permute-start(bf16[512,768]{1,0:T(8,128)(2,1)S(1)} %slice.399), channel_id=1, source_target_pairs={{0,1},{1,0},{2,3},{3,2},{4,5},{5,4},{6,7},{7,6},{8,9},{9,8},{10,11... | collective-permute-start | bytes 2359304 | tf_op jit(solution)/shard_map/ppermute | solution.py:186
  350.7 288.0 %copy-start.1 = (s32[2,1024]{1,0:T(2,128)S(1)}, s32[2,1024]{1,0:T(2,128)}, u32[]{:S(2)}) copy-start(s32[2,1024]{1,0:T(2,128)} %param.17) | copy-start | bytes 24580
  (27 other events, 46.5 us)
Sparse Core Ops, SparseCore 0:
  11.4 65.0 all-gather.7
  79.3 61.1 all-gather.9
  143.3 61.0 all-gather.11
  242.6 127.9 reduce-scatter.6
  376.1 127.6 reduce-scatter.8
  508.5 127.6 reduce-scatter.4

commit v2 on v1

--- a/solution.py
+++ b/solution.py
@@ -194,20 +194,149 @@
     return full[:rows] + swap(full[rows:].astype(BF16)).astype(F32)
 
 
-def gather_units(a):
+def flip(a, axis, bit):
+    n = lax.axis_size(axis)
+    return lax.ppermute(a, axis, [(i, i ^ bit) for i in range(n)])
+
+
+def double(a, axis, bit):
+    return jnp.concatenate([a, flip(a, axis, bit)], axis=0)
+
+
+def outer_bits(ndp):
+    return [1 << k for k in range(1, ndp.bit_length() - 1)]
+
+
+def gather_outer(a):
+    a = a[None]
+    for bit in outer_bits(lax.axis_size("dp")):
+        a = double(a, "dp", bit)
+    return a
+
+
+def gather_x_then_inner(a):
+    a = double(a, "x", 1)
+    return a, flip(a, "dp", 1)
+
+
+def gather_inner_then_x(a):
+    a = double(a, "dp", 1)
+    return a, flip(a, "x", 1)
+
+
+def pick(a, index, axis):
+    return lax.dynamic_index_in_dim(a, index, axis, keepdims=False)
+
+
+def add(a, b):
+    return (a.astype(F32) + b.astype(F32)).astype(BF16)
+
+
+def scatter_outer(a):
+    dp = lax.axis_index("dp")
+    bits = outer_bits(lax.axis_size("dp"))
+    for k, bit in reversed(list(enumerate(bits))):
+        half = a.shape[0] // 2
+        a = a.reshape(2, half, *a.shape[1:])
+        mine = (dp >> (k + 1)) & 1
+        sent = flip(pick(a, 1 - mine, 0), "dp", bit)
+        kept = pick(a, mine, 0)
+        a = add(kept, sent) if k else kept.astype(F32) + sent.astype(F32)
+    return a[0]
+
+
+def scatter_x_then_inner(own, other):
+    dp = lax.axis_index("dp")
+    a = add(own, flip(other, "x", 1))
+    return add(pick(a, dp & 1, 1), flip(pick(a, 1 - (dp & 1), 1), "dp", 1))
+
+
+def scatter_inner_then_x(own, other):
+    dp = lax.axis_index("dp")
+    a = jnp.stack([own, other])
+    a = add(pick(a, dp & 1, 2), flip(pick(a, 1 - (dp & 1), 2), "dp", 1))
+    return add(a[0], flip(a[1], "x", 1))
+
+
+def unit_places(count, x_major):
+    half = count // 2
+    nz = half // 2
+    places = []
+    for j in range(count):
+        late, early, z = j // half, (j % half) // nz, j % nz
+        rx, ry = (early, late) if x_major else (late, early)
+        places.append((2 * z + ry, rx))
+    return places
+
+
+def place_kernel(moves, out_count, dp_ref, *refs):
+    ins, outs = refs[:-out_count], refs[-out_count:]
+    dp = dp_ref[0]
+    for source, unit, rel, kind, rows_from, rows, cols_from, cols, target, col in moves:
+        value = ins[source][unit, rows_from : rows_from + rows, cols_from : cols_from + cols]
+        at = jnp.bitwise_xor(dp, rel)
+        if kind == "unit":
+            outs[target][at, :, col : col + cols] = value
+        else:
+            outs[target][pl.ds(pl.multiple_of(at * rows, 16), rows), col : col + cols] = value
+
+
+def place(pieces, moves, outs):
+    dp = lax.axis_index("dp").astype(jnp.int32)
     ndp = lax.axis_size("dp")
-    nx = lax.axis_size("x")
-    g = lax.all_gather(a, ("dp", "x"), axis=0, tiled=False)
-    g = g.reshape(ndp, nx, *a.shape)
-    return jnp.transpose(g, (1, 0, 2, 3)).reshape(nx, ndp * a.shape[0], a.shape[1])
-
-
-def scatter_units(g):
+    rows = min(m[5] for m in moves if m[3] == "rows")
+    if rows % 16 == 0:
+        whole = lambda s: pl.BlockSpec(s, lambda i, d: (0,) * len(s))
+        return pl.pallas_call(
+            functools.partial(place_kernel, moves, len(outs)),
+            grid_spec=pltpu.PrefetchScalarGridSpec(
+                num_scalar_prefetch=1,
+                grid=(1,),
+                in_specs=[whole(p.shape) for p in pieces],
+                out_specs=[whole(s) for s in outs],
+            ),
+            out_shape=[jax.ShapeDtypeStruct(s, BF16) for s in outs],
+            cost_estimate=pl.CostEstimate(flops=0, bytes_accessed=sum(2 * p.size * 2 for p in pieces), transcendentals=0),
+            name="place_units",
+        )(dp[None], *pieces)
+    made = []
+    for target, shape in enumerate(outs):
+        mine = [m for m in moves if m[8] == target]
+        columns = []
+        for col in sorted({m[9] for m in mine}):
+            units = sorted((m for m in mine if m[9] == col), key=lambda m: m[2])
+            stack = jnp.stack([pieces[m[0]][m[1], m[4] : m[4] + m[5], m[6] : m[6] + m[7]] for m in units])
+            stack = jnp.take(stack, jnp.bitwise_xor(jnp.arange(ndp), dp), axis=0)
+            columns.append(stack if mine[0][3] == "unit" else stack.reshape(-1, stack.shape[-1]))
+        made.append(jnp.concatenate(columns, axis=-1))
+    return made
+
+
+def place_wide(pieces, x_major, rows, cols, nx):
+    per = pieces[0].shape[0]
+    moves = []
+    for j, (rel, rx) in enumerate(unit_places(2 * per, x_major)):
+        moves.append((j // per, j % per, rel, "rows", 0, rows, 0, cols, 0, rx * cols))
+    return place(pieces, moves, [(rows * lax.axis_size("dp"), nx * cols)])[0]
+
+
+def place_attention(first, second, rows, part, nx):
     ndp = lax.axis_size("dp")
-    nx, model, cols = g.shape
-    g = g.reshape(nx, ndp, model // ndp, cols)
-    g = jnp.transpose(g, (1, 0, 2, 3)).reshape(ndp * nx * (model // ndp), cols)
-    return lax.psum_scatter(g, ("dp", "x"), scatter_dimension=0, tiled=True)
+    extra = first[0].shape[1] - rows
+    per = first[0].shape[0]
+    width = nx * part
+    moves = []
+    for j, (rel, rx) in enumerate(unit_places(2 * per, True)):
+        s, u = j // per, j % per
+        moves.append((s, u, rel, "rows", 0, rows, 0, part, 0, rx * part))
+        moves.append((s, u, rel, "rows", 0, rows, part, part, 0, width + rx * part))
+        moves.append((s, u, rel, "unit", rows, extra, 0, 2 * part, 2, rx * 2 * part))
+    for j, (rel, rx) in enumerate(unit_places(2 * per, False)):
+        s, u = 2 + j // per, j % per
+        moves.append((s, u, rel, "rows", 0, rows, 0, part, 0, 2 * width + rx * part))
+        moves.append((s, u, rel, "rows", 0, rows, part, part, 1, rx * part))
+    outs = [(rows * ndp, 3 * width), (rows * ndp, width), (ndp, extra, nx * 2 * part)]
+    return place([*first, *second], moves, outs)
 
 
 def local(
@@ -233,40 +362,43 @@
     seg_col = seg_rel[:, None]
     seg_row = seg_rel[None, :]
 
-    unit_a = jnp.concatenate([w_qkv[0], w_qkv[1], w_qkv[2], w_out.T], axis=1)
-    a_full = gather_units(unit_a)
-    b_full = gather_units(w_up)
-    c_full = gather_units(w_down.T)
     slim = model // (ndp * nx * 2)
+    qv = part // ndp
+    extra = 8
     small = jnp.concatenate(
-        [
-            b_out,
-            b_down,
-            g_one,
-            s_one,
-            g_two,
-            s_two,
-            b_qv.reshape(-1).astype(F32),
-            b_up.astype(F32),
-        ]
+        [b_out, b_down, g_one, s_one, g_two, s_two, b_qv.reshape(-1).astype(F32), b_up.astype(F32)]
     )
-    small = lax.all_gather(small, ("dp", "x", "c"), axis=0, tiled=False)
-    vectors = jnp.transpose(small[:, : 6 * slim].reshape(ndp * nx * 2, 6, slim), (1, 0, 2)).reshape(6, model)
+    high = small.astype(BF16)
+    middle = (small - high.astype(F32)).astype(BF16)
+    low = (small - high.astype(F32) - middle.astype(F32)).astype(BF16)
+    thirds = jnp.pad(jnp.stack([high, middle, low]), ((0, extra - 3), (0, 2 * part - small.shape[0])))
+    unit_qk = jnp.concatenate([jnp.concatenate([w_qkv[0], w_qkv[1]], axis=1), thirds], axis=0)
+    unit_vo = jnp.concatenate(
+        [jnp.concatenate([w_qkv[2], w_out.T], axis=1), jnp.zeros((extra, 2 * part), BF16)], axis=0
+    )
+    units = gather_outer(jnp.stack([unit_qk, unit_vo]))
+    qk_pieces = gather_x_then_inner(units[:, 0])
+    vo_pieces = gather_inner_then_x(units[:, 1])
+    w_all, o_t, ext = place_attention(qk_pieces, vo_pieces, piece, part, nx)
+    units = gather_outer(jnp.stack([w_up, w_down.T]))
+    b_all = place_wide(gather_x_then_inner(units[:, 0]), True, piece, model, nx)
+    c_all = place_wide(gather_inner_then_x(units[:, 1]), False, piece, model, nx)
+
+    ext = ext.astype(F32)
+    ext = (ext[:, 0] + ext[:, 1] + ext[:, 2]).reshape(ndp, nx, 2 * part)
+    six = ext[:, :, : 6 * slim]
+    six = jnp.stack([six, swap(six)], axis=2)
+    six = jnp.where(lax.broadcasted_iota(jnp.int32, (1, 1, 2, 1), 2) == parity, six[:, :, :1], six[:, :, 1:])
+    six = jnp.where(which == 0, six, six[:, ::-1]).reshape(ndp * nx * 2, 6, slim)
+    vectors = jnp.transpose(six, (1, 0, 2)).reshape(6, model)
     bout_f, bdown_f, gone_f, sone_f, gtwo_f, stwo_f = [vectors[i : i + 1] for i in range(6)]
-    wide = small[:, 6 * slim :].reshape(ndp, nx, 2, -1)
-    wide = lax.dynamic_index_in_dim(wide, parity, 2, keepdims=False)
-    qv = part // ndp
+    wide = ext[:, :, 6 * slim : 6 * slim + 2 * qv + piece]
     bias_qv = jnp.transpose(wide[:, :, : 2 * qv].reshape(ndp, nx, 2, qv), (2, 1, 0, 3)).reshape(2, width)
     bias_qkv = jnp.concatenate([bias_qv[0], jnp.zeros((width,), F32), bias_qv[1]])[None]
     bias_up = jnp.transpose(wide[:, :, 2 * qv :], (1, 0, 2)).reshape(1, nx * model)
 
     x_own = tokens
     x_full = pair_gather(x_own)
-    w_all = jnp.concatenate([a_full[i][:, j * part : (j + 1) * part] for j in range(3) for i in range(nx)], axis=1)
-    o_t = jnp.concatenate([a_full[i][:, 3 * part :] for i in range(nx)], axis=1)
-    b_all = jnp.concatenate([b_full[i] for i in range(nx)], axis=1)
-    c_all = jnp.concatenate([c_full[i] for i in range(nx)], axis=1)
-
     qkv = (dot_nn(x_full, w_all) + bias_qkv).astype(BF16)
     block = 256
     ctx, lse = attention_forward(qkv, seg_col, seg_row, block)
@@ -310,34 +442,44 @@
     grad_w = dot_tn(x_full, d_qkv).astype(BF16)
     input_grad = (d_first + pair_sum(dot_nt(d_qkv, w_all), rows)).astype(BF16)
 
-    unit_ga = jnp.stack(
-        [
-            jnp.concatenate(
-                [grad_w[:, j * width + i * part : j * width + (i + 1) * part] for j in range(3)]
-                + [grad_o[:, i * part : (i + 1) * part]],
-                axis=1,
-            )
-            for i in range(nx)
-        ]
+    split = lambda g, i: g[:, i * model : (i + 1) * model].reshape(ndp // 2, 2, piece, model)
+    got_c = scatter_x_then_inner(split(grad_c, 0), split(grad_c, 1))
+    got_b = scatter_inner_then_x(split(grad_b, 0), split(grad_b, 1))
+    got = scatter_outer(jnp.stack([got_c, got_b], axis=1))
+    gc, gb = got[0], got[1]
+
+    sums = jnp.stack([d_bias_out, d_bias_down, d_gain_one, d_shift_one, d_gain_two, d_shift_two])
+    sums = sums + swap(sums)
+    sums = jnp.transpose(sums.reshape(6, ndp, nx, 2, slim), (3, 2, 1, 0, 4))
+    sums = pick(sums, parity, 0).reshape(nx, ndp, 6 * slim)
+    sums = jnp.where(which == 0, sums, sums[::-1])
+    d_bqv = jnp.stack([d_bias_qkv[:width], d_bias_qkv[2 * width :]]).reshape(2, nx, ndp, qv)
+    d_bqv = jnp.transpose(d_bqv, (1, 2, 0, 3)).reshape(nx, ndp, 2 * qv)
+    d_bup = d_bias_up.reshape(nx, ndp, piece)
+    packed = jnp.concatenate([sums, d_bqv, d_bup], axis=-1).astype(BF16)
+    packed = jnp.pad(packed[:, :, None], ((0, 0), (0, 0), (0, extra - 1), (0, 2 * part - packed.shape[-1])))
+
+    def columns(g, j, i):
+        return g[:, j * width + i * part : j * width + (i + 1) * part]
+
+    def attention_unit(left, right, tail):
+        g = jnp.concatenate([left, right], axis=1).reshape(ndp, piece, 2 * part)
+        g = jnp.concatenate([g, tail], axis=1)
+        return g.reshape(ndp // 2, 2, piece + extra, 2 * part)
+
+    got_qk = scatter_x_then_inner(
+        *[attention_unit(columns(grad_w, 0, i), columns(grad_w, 1, i), packed[i]) for i in range(nx)]
     )
-    ga = scatter_units(unit_ga).astype(F32)
-    gb = scatter_units(jnp.stack([grad_b[:, i * model : (i + 1) * model] for i in range(nx)])).astype(F32)
-    gc = scatter_units(jnp.stack([grad_c[:, i * model : (i + 1) * model] for i in range(nx)])).astype(F32)
-    g_qkv = jnp.stack([ga[:, j * part : (j + 1) * part] for j in range(3)])
-    g_out = ga[:, 3 * part :].T
-
-    sums = jnp.stack([d_bias_out, d_bias_down, d_gain_one, d_shift_one, d_gain_two, d_shift_two])
-    sums = jnp.transpose(sums.reshape(6, ndp * nx * 2, slim), (1, 0, 2)).reshape(ndp, nx, 2, 6 * slim)
-    d_bqv = jnp.stack([d_bias_qkv[:width], d_bias_qkv[2 * width :]]).reshape(2, nx, ndp, qv)
-    d_bqv = jnp.transpose(d_bqv, (2, 1, 0, 3)).reshape(ndp, nx, 1, 2 * qv)
-    d_bup = jnp.transpose(d_bias_up.reshape(nx, ndp, piece), (1, 0, 2))[:, :, None]
-    tail = jnp.concatenate([d_bqv, d_bup], axis=-1)
-    tail = jnp.where(lax.broadcasted_iota(jnp.int32, (1, 1, 2, 1), 2) == parity, tail, 0.0)
-    packed = jnp.concatenate([sums, tail], axis=-1).reshape(ndp * nx * 2, -1)
-    mine = lax.psum_scatter(packed, ("dp", "x", "c"), scatter_dimension=0, tiled=True)[0]
+    got_vo = scatter_inner_then_x(
+        *[attention_unit(columns(grad_w, 2, i), columns(grad_o, 0, i), jnp.zeros_like(packed[i])) for i in range(nx)]
+    )
+    got = scatter_outer(jnp.stack([got_qk, got_vo], axis=1))
+    g_qkv = jnp.stack([got[0, :piece, :part], got[0, :piece, part:], got[1, :piece, :part]])
+    g_out = got[1, :piece, part:].T
+    mine = got[0, piece]
     six = [mine[i * slim : (i + 1) * slim] for i in range(6)]
     g_bqv = mine[6 * slim : 6 * slim + 2 * qv].reshape(2, qv)
-    g_bup = mine[6 * slim + 2 * qv :]
+    g_bup = mine[6 * slim + 2 * qv : 6 * slim + 2 * qv + piece]
     return (layer_out, input_grad, g_qkv, g_bqv, g_out, gb, g_bup, gc.T, *six)
 
 

time: 656 us -> 327 us (0.50)
  waiting for transfers between devices: 390 us -> 120 us
  blocking collectives: 85.6 us -> 0 us
  starting transfers between devices: 1.79 us -> 31.4 us
  between operations: 15.5 us -> 1.81 us
  Pallas kernels: 35.8 us -> 45.8 us
  other arithmetic: 25.7 us -> 34.4 us
    reduce_scatter x3 -> x0, waiting for transfers between devices: 279 us -> none  [scatter_units(): return lax.psum_scatter(g, ('dp', 'x'), scatter_dimension=0, tiled=True)]
    ppermute x0 -> x24, waiting for transfers between devices: none -> 117 us  [flip(): return lax.ppermute(a, axis, [(i, i ^ bit) for i in range(n)])]
    all_gather x3 -> x0, waiting for transfers between devices: 104 us -> none  [gather_units(): g = lax.all_gather(a, ('dp', 'x'), axis=0, tiled=False)]
    unnamed x2 -> x0, blocking collectives: 85.6 us -> none
    ppermute x0 -> x24, starting transfers between devices: none -> 29.8 us  [flip(): return lax.ppermute(a, axis, [(i, i ^ bit) for i in range(n)])]
    pallas_call x0 -> x3, Pallas kernels: none -> 10 us  [place(): pl.pallas_call(functools.partial(place_kernel, moves, len(outs)), grid_sp...]
  transfers between devices with their start and end apart: 14 -> 34, of which waited for: 10 -> 17; matrix products, arithmetic and copies ran while one was open for 12% -> 24% of each run, Pallas kernels for 6% -> 14%
where the time goes in v2:
time: 327 us; the launch traced here: 322 us
  waiting for transfers between devices  120 us (37%)
  matrix products  51.6 us (16%)
  Pallas kernels  45.8 us (14%)
  local copies, waits for them, and re-layouts  37.1 us (11%)
  other arithmetic  34.4 us (11%)
  starting transfers between devices  31.4 us (10%)
    ppermute x24, waiting for transfers between devices, flip(): return lax.ppermute(a, axis, [(i, i ^ bit) for i in range(n)])  117 us
    dot_general x12, matrix products, dot(): return lax.dot_general(a, b, (dims, ((), ())), preferred_element_type=F32)  51.6 us
    ppermute x24, starting transfers between devices, flip(): return lax.ppermute(a, axis, [(i, i ^ bit) for i in range(n)])  29.8 us
    pallas_call x1, Pallas kernels, attention_backward(): pl.pallas_call(functools.partial(attention_backward_kernel, width), grid=...  20.4 us
    pallas_call x1, Pallas kernels, attention_forward(): pl.pallas_call(functools.partial(attention_forward_kernel, width), grid=(...  15.4 us
    unnamed x93, local copies, waits for them, and re-layouts  10.9 us
    pallas_call x3, Pallas kernels, place(): pl.pallas_call(functools.partial(place_kernel, moves, len(outs)), grid_sp...  10 us
    convert_element_type x10, other arithmetic, add(): return (a.astype(F32) + b.astype(F32)).astype(BF16)  7.89 us
  transfers between devices with their start and end apart: 34, of which 17 were waited for; matrix products, arithmetic and copies ran while one was open for 24% of the time, Pallas kernels for 14%

profile of v2, /device:TPU:0, one launch (start us, length us, event | category | flops | bytes accessed | tf_op | source)
XLA Modules:
  0.0 322.2 jit_solution(14259197988265408728)
XLA Ops:
  4.9 3.1 collective-permute-start.1
  8.0 4.1 %collective-permute-done.1 = bf16[1,2,104,384]{3,2,0,1:T(8,128)(2,1)S(1)} collective-permute-done((bf16[1,2,104,384]{3,2,0,1:T(8,128)(2,1)S(1)}, bf16[1,2,104,384]{3,2,0,1:T(8,128)(2,1)S(1)}, u32[]{:S(2)}, u32[]{:S(2)}) %collective-permute-start.1) | collective-permute-done | bytes 159776 | tf_op jit(solution)/shard_map/ppermute | solution.py:199
  12.2 2.8 collective-permute-start.2
  16.7 12.0 %collective-permute-done.2 = bf16[2,2,104,384]{3,2,0,1:T(8,128)(2,1)S(1)} collective-permute-done((bf16[2,2,104,384]{3,2,0,1:T(8,128)(2,1)S(1)}, bf16[2,2,104,384]{3,2,0,1:T(8,128)(2,1)S(1)}, u32[]{:S(2)}, u32[]{:S(2)}) %collective-permute-start.2) | collective-permute-done | bytes 319520 | tf_op jit(solution)/shard_map/ppermute | solution.py:199
  33.1 4.4 %collective-permute-done.3 = bf16[4,104,384]{2,1,0:T(8,128)(2,1)S(1)} collective-permute-done((bf16[4,104,384]{2,1,0:T(8,128)(2,1)S(1)}, bf16[4,104,384]{2,1,0:T(8,128)(2,1)S(1)}, u32[]{:S(2)}, u32[]{:S(2)}) %collective-permute-start.3) | collective-permute-done | bytes 319520 | tf_op jit(solution)/shard_map/ppermute | solution.py:199
  43.6 16.5 %collective-permute-done.11 = bf16[2,2,96,768]{3,2,0,1:T(8,128)(2,1)S(1)} collective-permute-done((bf16[2,2,96,768]{3,2,0,1:T(8,128)(2,1)S(1)}, bf16[2,2,96,768]{3,2,0,1:T(8,128)(2,1)S(1)}, u32[]{:S(2)}, u32[]{:S(2)}) %collective-permute-start.11) | collective-permute-done | bytes 589856 | tf_op jit(solution)/shard_map/ppermute | solution.py:199
  64.2 3.6 %place_units.3 = (bf16[768,1152]{1,0:T(8,128)(2,1)}, bf16[768,384]{1,0:T(8,128)(2,1)}, bf16[8,8,768]{2,1,0:T(8,128)(2,1)}) custom-call(s32[1]{0:T(128)} %bitcast.4.dp_ref, bf16[8,104,384]{2,1,0:T(8,128)(2,1)} %copy-done.14, bf16[8,104,384]{2,1,0:T(8,128)(2,1)} %copy-done.26, bf16[8,104,384]{2,1,0:T(8,128)(2,1)} %copy-done.15, bf16[8,104,384]{2,1,0:T(8,128)(2,1)} %copy-done.27), custom_call_target="tpu_custom_call" | custom-call | bytes 5111808 | tf_op jit(solution)/shard_map/place_units/pallas_call | solution.py:290
  70.0 5.1 %add_convert_fusion.q_ref.k_ref.v_ref = bf16[1024,1152]{1,0:T(8,128)(2,1)} fusion(bf16[1024,768]{1,0:T(8,128)(2,1)S(1)} %copy-done.31, bf16[768,1152]{1,0:T(8,128)(2,1)} %get-tuple-element.19, f32[1152]{0:T(1024)S(1)} %pad_maximum_fusion.23), kind=kOutput, calls=%fused_computation.9 | convolution fusion | flops 1814298624 | bytes 5706240 | tf_op jit(solution)/shard_map/dot_general | solution.py:20
  75.2 15.4 %attention_forward.1 = (bf16[1024,384]{1,0:T(8,128)(2,1)}, f32[8,1024]{1,0:T(8,128)}) custom-call(s32[1024,1]{1,0:T(8,128)} %copy.77.seg_q_ref.seg_k_ref, s32[1,1024]{1,0:T(1,128)} %bitcast.183, bf16[1024,1152]{1,0:T(8,128)(2,1)} %add_convert_fusion.q_ref.k_ref.v_ref, bf16[1024,1152]{1,0:T(8,128)(2,1)} %add_convert_fusion.q_ref.k_ref.v_ref, ...), custom_call_target="tpu_custom_call" | custom-call | flops 6442450944 | bytes 3145728 | tf_op jit(solution)/shard_map/attention_forward/pallas_call | solution.py:63
  108.6 17.8 %collective-permute-done.13.refs_1_ = bf16[8,96,768]{2,1,0:T(8,128)(2,1)} collective-permute-done((bf16[8,96,768]{2,1,0:T(8,128)(2,1)S(1)}, bf16[8,96,768]{2,1,0:T(8,128)(2,1)}, u32[]{:S(2)}, u32[]{:S(2)}) %collective-permute-start.13) | collective-permute-done | bytes 1179680 | tf_op jit(solution)/shard_map/ppermute | solution.py:199
  126.5 3.2 place_units.4
  130.0 3.2 place_units.5
  133.2 6.8 %multiply_convert_fusion.1 = (bf16[1024,1536]{1,0:T(8,128)(2,1)S(1)}, f32[1024,1536]{1,0:T(8,128)}) fusion(f32[1536]{0:T(1024)S(1)} %copy-done.39, bf16[768,1536]{1,0:T(8,128)(2,1)} %place_units.4, bf16[512,768]{1,0:T(8,128)(2,1)} %collective-permute-done.9, bf16[512,768]{1,0:T(8,128)(2,1)S(1)} %fusion.21), kind=kOutput, calls=%fused_computation.7 | convolution fusion | flops 2428502016 | bytes 13375488 | tf_op jit(solution)/shard_map/dot_general | solution.py:20
  140.1 2.6 fusion.95
  155.3 8.6 %fusion.93 = (bf16[1536]{0:T(1024)(128)(2,1)}, bf16[1024,1536]{1,0:T(8,128)(2,1)S(1)}) fusion(f32[1024,1536]{1,0:T(8,128)} %get-tuple-element.162, f32[1536]{0:T(1024)S(1)} %copy-done.40, bf16[768,1536]{1,0:T(8,128)(2,1)} %place_units.5, bf16[512,768]{1,0:T(8,128)(2,1)} %collective-permute-done.17, bf16[512,768]{1,0:T(8,128)(2,1)} %get-tuple-element.117), kind=kOutput, calls=%fused_computation.236 | convolution fusion | flops 2441083392 | bytes 13378560 | tf_op jit(solution)/shard_map/dot_general | solution.py:20
  163.9 2.6 fusion.96
  166.6 4.1 %convolution_convert_fusion = bf16[768,1536]{1,0:T(8,128)(2,1)S(1)} fusion(bf16[1024,1536]{1,0:T(8,128)(2,1)S(1)} %get-tuple-element.164, bf16[512,768]{1,0:T(8,128)(2,1)} %collective-permute-done.9, bf16[512,768]{1,0:T(8,128)(2,1)S(1)} %copy-done.23), kind=kOutput, calls=%fused_computation.10 | convolution fusion | flops 2420244480 | bytes 7077888 | tf_op jit(solution)/shard_map/dot_general | solution.py:20
  174.0 4.3 %convolution_convert_fusion.1 = bf16[768,1536]{1,0:T(8,128)(2,1)S(1)} fusion(bf16[1024,1536]{1,0:T(8,128)(2,1)S(1)} %copy-done.43, bf16[512,768]{1,0:T(8,128)(2,1)} %collective-permute-done.17, bf16[512,768]{1,0:T(8,128)(2,1)} %get-tuple-element.117), kind=kOutput, calls=%fused_computation.11 | convolution fusion | flops 2420244480 | bytes 7077888 | tf_op jit(solution)/shard_map/dot_general | solution.py:20
  188.6 12.3 %collective-permute-done.30 = bf16[2,4,96,768]{3,2,1,0:T(8,128)(2,1)} collective-permute-done((bf16[2,4,96,768]{3,2,1,0:T(8,128)(2,1)}, bf16[2,4,96,768]{3,2,1,0:T(8,128)(2,1)}, u32[]{:S(2)}, u32[]{:S(2)}) %collective-permute-start.30) | collective-permute-done | bytes 1179680 | tf_op jit(solution)/shard_map/ppermute | solution.py:199
  205.0 4.0 %collective-permute-done.28 = bf16[4,2,96,768]{3,2,1,0:T(8,128)(2,1)} collective-permute-done((bf16[4,2,96,768]{3,2,1,0:T(8,128)(2,1)}, bf16[4,2,96,768]{3,2,1,0:T(8,128)(2,1)}, u32[]{:S(2)}, u32[]{:S(2)}) %collective-permute-start.28) | collective-permute-done | bytes 1179680 | tf_op jit(solution)/shard_map/ppermute | solution.py:199
  212.4 3.0 convolution_convert_fusion.3.d_ref
  215.4 20.4 %attention_backward.1 = bf16[1024,1152]{1,0:T(8,128)(2,1)} custom-call(s32[1024,1]{1,0:T(8,128)} %copy.77.seg_q_ref.seg_k_ref, s32[1,1024]{1,0:T(1,128)} %bitcast.184, bf16[1024,1152]{1,0:T(8,128)(2,1)} %add_convert_fusion.q_ref.k_ref.v_ref, bf16[1024,1152]{1,0:T(8,128)(2,1)} %add_convert_fusion.q_ref.k_ref.v_ref, ...), custom_call_target="tpu_custom_call" | custom-call | flops 16106127360 | bytes 6291456 | tf_op jit(solution)/shard_map/attention_backward/pallas_call | solution.py:145
  235.9 5.8 %convolution_convert_fusion.2 = bf16[768,1152]{1,0:T(8,128)(2,1)} fusion(bf16[1024,768]{1,0:T(8,128)(2,1)} %copy-done.30, bf16[1024,1152]{1,0:T(8,128)(2,1)} %attention_backward.1), kind=kOutput, calls=%fused_computation.12 | convolution fusion | flops 1812824064 | bytes 5701632 | tf_op jit(solution)/shard_map/dot_general | solution.py:20
  241.7 3.9 %fusion.97 = f32[1024,768]{1,0:T(8,128)} fusion(bf16[1024,1152]{1,0:T(8,128)(2,1)S(1)} %copy-done.18, bf16[768,1152]{1,0:T(8,128)(2,1)S(1)} %copy-done.41), kind=kOutput, calls=%fused_computation.240 | convolution fusion | flops 1811939328 | bytes 7274496 | tf_op jit(solution)/shard_map/dot_general | solution.py:20
  248.1 2.5 convolution_convert_fusion.4
  260.4 6.2 %collective-permute-done.24 = bf16[2,4,104,384]{3,2,1,0:T(8,128)(2,1)S(1)} collective-permute-done((bf16[2,4,104,384]{3,2,1,0:T(8,128)(2,1)S(1)}, bf16[2,4,104,384]{3,2,1,0:T(8,128)(2,1)S(1)}, u32[]{:S(2)}, u32[]{:S(2)}) %collective-permute-start.24) | collective-permute-done | bytes 639008 | tf_op jit(solution)/shard_map/ppermute | solution.py:199
  269.8 18.4 %collective-permute-done.32 = bf16[2,2,96,768]{3,2,1,0:T(8,128)(2,1)S(1)} collective-permute-done((bf16[2,2,96,768]{3,2,1,0:T(8,128)(2,1)S(1)}, bf16[2,2,96,768]{3,2,1,0:T(8,128)(2,1)S(1)}, u32[]{:S(2)}, u32[]{:S(2)}) %collective-permute-start.32) | collective-permute-done | bytes 589856 | tf_op jit(solution)/shard_map/ppermute | solution.py:199
  291.0 3.3 %collective-permute-start.26 = (bf16[2,2,104,384]{2,3,1,0:T(8,128)(2,1)S(1)}, bf16[2,2,104,384]{2,3,1,0:T(8,128)(2,1)S(1)}, u32[]{:S(2)}, u32[]{:S(2)}) collective-permute-start(bf16[2,2,104,384]{2,3,1,0:T(8,128)(2,1)S(1)} %fusion.43), channel_id=1, source_target_pairs={{0,16},{4,20},{8,24},{12,28},{16,0},{20,4},{24,8},{28,12},{1,17},{... | collective-permute-start | bytes 958472 | tf_op jit(solution)/shard_map/ppermute | solution.py:199
  294.2 2.8 fusion.15
  297.1 5.7 %collective-permute-done.33 = bf16[1,2,96,768]{3,2,1,0:T(8,128)(2,1)} collective-permute-done((bf16[1,2,96,768]{3,2,1,0:T(8,128)(2,1)}, bf16[1,2,96,768]{3,2,1,0:T(8,128)(2,1)}, u32[]{:S(2)}, u32[]{:S(2)}) %collective-permute-start.33) | collective-permute-done | bytes 294944 | tf_op jit(solution)/shard_map/ppermute | solution.py:199
  303.8 7.9 %collective-permute-done.26 = bf16[2,2,104,384]{2,3,1,0:T(8,128)(2,1)S(1)} collective-permute-done((bf16[2,2,104,384]{2,3,1,0:T(8,128)(2,1)S(1)}, bf16[2,2,104,384]{2,3,1,0:T(8,128)(2,1)S(1)}, u32[]{:S(2)}, u32[]{:S(2)}) %collective-permute-start.26) | collective-permute-done | bytes 319520 | tf_op jit(solution)/shard_map/ppermute | solution.py:199
  312.9 5.2 %collective-permute-done.27 = bf16[1,2,104,384]{2,3,1,0:T(8,128)(2,1)S(1)} collective-permute-done((bf16[1,2,104,384]{2,3,1,0:T(8,128)(2,1)S(1)}, bf16[1,2,104,384]{2,3,1,0:T(8,128)(2,1)S(1)}, u32[]{:S(2)}, u32[]{:S(2)}) %collective-permute-start.27) | collective-permute-done | bytes 159776 | tf_op jit(solution)/shard_map/ppermute | solution.py:199
  (284 shorter events, 98.5 us)
Async XLA Ops:
  4.9 7.2 %collective-permute-start.1 = (bf16[1,2,104,384]{3,2,0,1:T(8,128)(2,1)S(1)}, bf16[1,2,104,384]{3,2,0,1:T(8,128)(2,1)S(1)}, u32[]{:S(2)}, u32[]{:S(2)}) collective-permute-start(bf16[1,2,104,384]{3,2,0,1:T(8,128)(2,1)S(1)} %maximum_bitcast_fusion.1), channel_id=1, source_target_pairs={{0,8},{4,12},{8,0},{12,4},{16,24},{20,28},{24,16},{28,20},{1,9},{5... | collective-permute-start | bytes 479240 | tf_op jit(solution)/shard_map/ppermute | solution.py:199
  12.2 16.5 %collective-permute-start.2 = (bf16[2,2,104,384]{3,2,0,1:T(8,128)(2,1)S(1)}, bf16[2,2,104,384]{3,2,0,1:T(8,128)(2,1)S(1)}, u32[]{:S(2)}, u32[]{:S(2)}) collective-permute-start(bf16[2,2,104,384]{3,2,0,1:T(8,128)(2,1)S(1)} %pad_maximum_fusion.21), channel_id=1, source_target_pairs={{0,16},{4,20},{8,24},{12,28},{16,0},{20,4},{24,8},{28,12},{1,17},{... | collective-permute-start | bytes 958472 | tf_op jit(solution)/shard_map/ppermute | solution.py:199
  15.0 17.8 %collective-permute-start.10 = (bf16[1,2,96,768]{3,2,0,1:T(8,128)(2,1)S(1)}, bf16[1,2,96,768]{3,2,0,1:T(8,128)(2,1)S(1)}, u32[]{:S(2)}, u32[]{:S(2)}) collective-permute-start(bf16[1,2,96,768]{3,2,0,1:T(8,128)(2,1)S(1)} %maximum_bitcast_fusion), channel_id=1, source_target_pairs={{0,8},{4,12},{8,0},{12,4},{16,24},{20,28},{24,16},{28,20},{1,9},{5... | collective-permute-start | bytes 884744 | tf_op jit(solution)/shard_map/ppermute | solution.py:199
  16.7 24.5 %collective-permute-start = (bf16[512,768]{1,0:T(8,128)(2,1)S(1)}, bf16[512,768]{1,0:T(8,128)(2,1)}, u32[]{:S(2)}, u32[]{:S(2)}) collective-permute-start(bf16[512,768]{1,0:T(8,128)(2,1)S(1)} %copy-done.12), channel_id=1, source_target_pairs={{0,1},{1,0},{2,3},{3,2},{4,5},{5,4},{6,7},{7,6},{8,9},{9,8},{10,11... | collective-permute-start | bytes 2359304 | tf_op jit(solution)/shard_map/ppermute | solution.py:186
  28.9 8.6 %collective-permute-start.3 = (bf16[4,104,384]{2,1,0:T(8,128)(2,1)S(1)}, bf16[4,104,384]{2,1,0:T(8,128)(2,1)S(1)}, u32[]{:S(2)}, u32[]{:S(2)}) collective-permute-start(bf16[4,104,384]{2,1,0:T(8,128)(2,1)S(1)} %get-tuple-element.140), channel_id=1, source_target_pairs={{0,2},{2,0},{1,3},{3,1},{4,6},{6,4},{5,7},{7,5},{8,10},{10,8},{9,1... | collective-permute-start | bytes 958472 | tf_op jit(solution)/shard_map/ppermute | solution.py:199
  31.3 9.1 %collective-permute-start.5 = (bf16[4,104,384]{2,1,0:T(8,128)(2,1)S(1)}, bf16[4,104,384]{2,1,0:T(8,128)(2,1)S(1)}, u32[]{:S(2)}, u32[]{:S(2)}) collective-permute-start(bf16[4,104,384]{2,1,0:T(8,128)(2,1)S(1)} %get-tuple-element.139), channel_id=1, source_target_pairs={{0,4},{4,0},{8,12},{12,8},{16,20},{20,16},{24,28},{28,24},{1,5},{5... | collective-permute-start | bytes 958472 | tf_op jit(solution)/shard_map/ppermute | solution.py:199
  32.9 27.2 %collective-permute-start.11 = (bf16[2,2,96,768]{3,2,0,1:T(8,128)(2,1)S(1)}, bf16[2,2,96,768]{3,2,0,1:T(8,128)(2,1)S(1)}, u32[]{:S(2)}, u32[]{:S(2)}) collective-permute-start(bf16[2,2,96,768]{3,2,0,1:T(8,128)(2,1)S(1)} %pad_maximum_fusion.16), channel_id=1, source_target_pairs={{0,16},{4,20},{8,24},{12,28},{16,0},{20,4},{24,8},{28,12},{1,17},{... | collective-permute-start | bytes 1769480 | tf_op jit(solution)/shard_map/ppermute | solution.py:199
  37.6 25.0 %collective-permute-start.4 = (bf16[8,104,384]{2,1,0:T(8,128)(2,1)S(1)}, bf16[8,104,384]{2,1,0:T(8,128)(2,1)S(1)}, u32[]{:S(2)}, u32[]{:S(2)}) collective-permute-start(bf16[8,104,384]{2,1,0:T(8,128)(2,1)S(1)} %pad_maximum_fusion.13.refs_0_), channel_id=1, source_target_pairs={{0,4},{4,0},{8,12},{12,8},{16,20},{20,16},{24,28},{28,24},{1,5},{5... | collective-permute-start | bytes 1916936 | tf_op jit(solution)/shard_map/ppermute | solution.py:199
  40.5 22.0 %collective-permute-start.6 = (bf16[8,104,384]{2,1,0:T(8,128)(2,1)S(1)}, bf16[8,104,384]{2,1,0:T(8,128)(2,1)S(1)}, u32[]{:S(2)}, u32[]{:S(2)}) collective-permute-start(bf16[8,104,384]{2,1,0:T(8,128)(2,1)S(1)} %pad_maximum_fusion.14.refs_2_), channel_id=1, source_target_pairs={{0,2},{2,0},{1,3},{3,1},{4,6},{6,4},{5,7},{7,5},{8,10},{10,8},{9,1... | collective-permute-start | bytes 1916936 | tf_op jit(solution)/shard_map/ppermute | solution.py:199
  61.2 38.5 %collective-permute-start.14 = (bf16[4,96,768]{2,1,0:T(8,128)(2,1)}, bf16[4,96,768]{2,1,0:T(8,128)(2,1)}, u32[]{:S(2)}, u32[]{:S(2)}) collective-permute-start(bf16[4,96,768]{2,1,0:T(8,128)(2,1)} %get-tuple-element.137), channel_id=1, source_target_pairs={{0,4},{4,0},{8,12},{12,8},{16,20},{20,16},{24,28},{28,24},{1,5},{5... | collective-permute-start | bytes 1769480 | tf_op jit(solution)/shard_map/ppermute | solution.py:199
  61.7 35.4 %collective-permute-start.12 = (bf16[4,96,768]{2,1,0:T(8,128)(2,1)S(1)}, bf16[4,96,768]{2,1,0:T(8,128)(2,1)}, u32[]{:S(2)}, u32[]{:S(2)}) collective-permute-start(bf16[4,96,768]{2,1,0:T(8,128)(2,1)S(1)} %get-tuple-element.138), channel_id=1, source_target_pairs={{0,2},{2,0},{1,3},{3,1},{4,6},{6,4},{5,7},{7,5},{8,10},{10,8},{9,1... | collective-permute-start | bytes 1769480 | tf_op jit(solution)/shard_map/ppermute | solution.py:199
  69.9 25.1 %collective-permute-start.8 = (f32[8,2,144]{2,1,0:T(2,128)}, f32[8,2,144]{2,1,0:T(2,128)}, u32[]{:S(2)}, u32[]{:S(2)}) collective-permute-start(f32[8,2,144]{2,1,0:T(2,128)} %slice.331), channel_id=1, source_target_pairs={{0,1},{1,0},{2,3},{3,2},{4,5},{5,4},{6,7},{7,6},{8,9},{9,8},{10,11... | collective-permute-start | bytes 27656 | tf_op jit(solution)/shard_map/ppermute | solution.py:186
  94.5 9.1 %collective-permute-start.7 = (bf16[512,768]{1,0:T(8,128)(2,1)S(1)}, bf16[512,768]{1,0:T(8,128)(2,1)}, u32[]{:S(2)}, u32[]{:S(2)}) collective-permute-start(bf16[512,768]{1,0:T(8,128)(2,1)S(1)} %slice.447), channel_id=1, source_target_pairs={{0,1},{1,0},{2,3},{3,2},{4,5},{5,4},{6,7},{7,6},{8,9},{9,8},{10,11... | collective-permute-start | bytes 2359304 | tf_op jit(solution)/shard_map/ppermute | solution.py:186
  98.4 28.1 %collective-permute-start.13 = (bf16[8,96,768]{2,1,0:T(8,128)(2,1)S(1)}, bf16[8,96,768]{2,1,0:T(8,128)(2,1)}, u32[]{:S(2)}, u32[]{:S(2)}) collective-permute-start(bf16[8,96,768]{2,1,0:T(8,128)(2,1)S(1)} %pad_maximum_fusion.4.refs_0_), channel_id=1, source_target_pairs={{0,4},{4,0},{8,12},{12,8},{16,20},{20,16},{24,28},{28,24},{1,5},{5... | collective-permute-start | bytes 3538952 | tf_op jit(solution)/shard_map/ppermute | solution.py:199
  102.1 27.9 %collective-permute-start.15 = (bf16[8,96,768]{2,1,0:T(8,128)(2,1)}, bf16[8,96,768]{2,1,0:T(8,128)(2,1)}, u32[]{:S(2)}, u32[]{:S(2)}) collective-permute-start(bf16[8,96,768]{2,1,0:T(8,128)(2,1)} %pad_maximum_fusion.5.refs_0_), channel_id=1, source_target_pairs={{0,2},{2,0},{1,3},{3,1},{4,6},{6,4},{5,7},{7,5},{8,10},{10,8},{9,1... | collective-permute-start | bytes 3538952 | tf_op jit(solution)/shard_map/ppermute | solution.py:199
  105.8 27.4 %collective-permute-start.9 = (bf16[512,768]{1,0:T(8,128)(2,1)S(1)}, bf16[512,768]{1,0:T(8,128)(2,1)}, u32[]{:S(2)}, u32[]{:S(2)}) collective-permute-start(bf16[512,768]{1,0:T(8,128)(2,1)S(1)} %fusion.21), channel_id=1, source_target_pairs={{0,1},{1,0},{2,3},{3,2},{4,5},{5,4},{6,7},{7,6},{8,9},{9,8},{10,11... | collective-permute-start | bytes 2359304 | tf_op jit(solution)/shard_map/ppermute | solution.py:186
  152.6 2.6 collective-permute-start.17
  170.9 10.4 %collective-permute-start.18 = (bf16[512,768]{1,0:T(8,128)(2,1)S(1)}, bf16[512,768]{1,0:T(8,128)(2,1)S(1)}, u32[]{:S(2)}, u32[]{:S(2)}) collective-permute-start(bf16[512,768]{1,0:T(8,128)(2,1)S(1)} %slice.445), channel_id=1, source_target_pairs={{0,1},{1,0},{2,3},{3,2},{4,5},{5,4},{6,7},{7,6},{8,9},{9,8},{10,11... | collective-permute-start | bytes 2359304 | tf_op jit(solution)/shard_map/ppermute | solution.py:186
  172.6 28.3 %collective-permute-start.30 = (bf16[2,4,96,768]{3,2,1,0:T(8,128)(2,1)}, bf16[2,4,96,768]{3,2,1,0:T(8,128)(2,1)}, u32[]{:S(2)}, u32[]{:S(2)}) collective-permute-start(bf16[2,4,96,768]{3,2,1,0:T(8,128)(2,1)} %fusion.24), channel_id=1, source_target_pairs={{0,4},{4,0},{8,12},{12,8},{16,20},{20,16},{24,28},{28,24},{1,5},{5... | collective-permute-start | bytes 3538952 | tf_op jit(solution)/shard_map/ppermute | solution.py:199
  179.9 29.1 %collective-permute-start.28 = (bf16[4,2,96,768]{3,2,1,0:T(8,128)(2,1)}, bf16[4,2,96,768]{3,2,1,0:T(8,128)(2,1)}, u32[]{:S(2)}, u32[]{:S(2)}) collective-permute-start(bf16[4,2,96,768]{3,2,1,0:T(8,128)(2,1)} %bitcast.55), channel_id=1, source_target_pairs={{0,2},{2,0},{1,3},{3,1},{4,6},{6,4},{5,7},{7,5},{8,10},{10,8},{9,1... | collective-permute-start | bytes 3538952 | tf_op jit(solution)/shard_map/ppermute | solution.py:199
  187.8 24.7 %collective-permute-start.19 = (bf16[512,768]{1,0:T(8,128)(2,1)S(1)}, bf16[512,768]{1,0:T(8,128)(2,1)}, u32[]{:S(2)}, u32[]{:S(2)}) collective-permute-start(bf16[512,768]{1,0:T(8,128)(2,1)S(1)} %get-tuple-element.119), channel_id=1, source_target_pairs={{0,1},{1,0},{2,3},{3,2},{4,5},{5,4},{6,7},{7,6},{8,9},{9,8},{10,11... | collective-permute-start | bytes 2359304 | tf_op jit(solution)/shard_map/ppermute | solution.py:186
  203.6 54.2 %collective-permute-start.31 = (bf16[4,96,768]{2,1,0:T(8,128)(2,1)}, bf16[4,96,768]{2,1,0:T(8,128)(2,1)}, u32[]{:S(2)}, u32[]{:S(2)}) collective-permute-start(bf16[4,96,768]{2,1,0:T(8,128)(2,1)} %slice_bitcast_fusion), channel_id=1, source_target_pairs={{0,2},{2,0},{1,3},{3,1},{4,6},{6,4},{5,7},{7,5},{8,10},{10,8},{9,1... | collective-permute-start | bytes 1769480 | tf_op jit(solution)/shard_map/ppermute | solution.py:199
  211.6 47.4 %collective-permute-start.29 = (bf16[4,96,768]{2,1,0:T(8,128)(2,1)}, bf16[4,96,768]{2,1,0:T(8,128)(2,1)}, u32[]{:S(2)}, u32[]{:S(2)}) collective-permute-start(bf16[4,96,768]{2,1,0:T(8,128)(2,1)} %dynamic-slice_bitcast_fusion), channel_id=1, source_target_pairs={{0,4},{4,0},{8,12},{12,8},{16,20},{20,16},{24,28},{28,24},{1,5},{5... | collective-permute-start | bytes 1769480 | tf_op jit(solution)/shard_map/ppermute | solution.py:199
  252.0 14.5 %collective-permute-start.24 = (bf16[2,4,104,384]{3,2,1,0:T(8,128)(2,1)S(1)}, bf16[2,4,104,384]{3,2,1,0:T(8,128)(2,1)S(1)}, u32[]{:S(2)}, u32[]{:S(2)}) collective-permute-start(bf16[2,4,104,384]{3,2,1,0:T(8,128)(2,1)S(1)} %fusion.33), channel_id=1, source_target_pairs={{0,4},{4,0},{8,12},{12,8},{16,20},{20,16},{24,28},{28,24},{1,5},{5... | collective-permute-start | bytes 1916936 | tf_op jit(solution)/shard_map/ppermute | solution.py:199
  253.6 15.3 %collective-permute-start.22 = (bf16[4,2,104,384]{3,2,1,0:T(8,128)(2,1)S(1)}, bf16[4,2,104,384]{3,2,1,0:T(8,128)(2,1)S(1)}, u32[]{:S(2)}, u32[]{:S(2)}) collective-permute-start(bf16[4,2,104,384]{3,2,1,0:T(8,128)(2,1)S(1)} %pad_maximum_fusion.15), channel_id=1, source_target_pairs={{0,2},{2,0},{1,3},{3,1},{4,6},{6,4},{5,7},{7,5},{8,10},{10,8},{9,1... | collective-permute-start | bytes 1916936 | tf_op jit(solution)/shard_map/ppermute | solution.py:199
  257.5 36.7 %collective-permute-start.20 = (bf16[512,768]{1,0:T(8,128)(2,1)}, bf16[512,768]{1,0:T(8,128)(2,1)}, u32[]{:S(2)}, u32[]{:S(2)}) collective-permute-start(bf16[512,768]{1,0:T(8,128)(2,1)} %slice.444), channel_id=1, source_target_pairs={{0,1},{1,0},{2,3},{3,2},{4,5},{5,4},{6,7},{7,6},{8,9},{9,8},{10,11... | collective-permute-start | bytes 2359304 | tf_op jit(solution)/shard_map/ppermute | solution.py:186
  260.3 27.9 %collective-permute-start.32 = (bf16[2,2,96,768]{3,2,1,0:T(8,128)(2,1)S(1)}, bf16[2,2,96,768]{3,2,1,0:T(8,128)(2,1)S(1)}, u32[]{:S(2)}, u32[]{:S(2)}) collective-permute-start(bf16[2,2,96,768]{3,2,1,0:T(8,128)(2,1)S(1)} %fusion.39), channel_id=1, source_target_pairs={{0,16},{4,20},{8,24},{12,28},{16,0},{20,4},{24,8},{28,12},{1,17},{... | collective-permute-start | bytes 1769480 | tf_op jit(solution)/shard_map/ppermute | solution.py:199
  266.8 22.3 %collective-permute-start.25 = (bf16[4,104,384]{2,1,0:T(8,128)(2,1)S(1)}, bf16[4,104,384]{2,1,0:T(8,128)(2,1)S(1)}, u32[]{:S(2)}, u32[]{:S(2)}) collective-permute-start(bf16[4,104,384]{2,1,0:T(8,128)(2,1)S(1)} %slice_bitcast_fusion.4), channel_id=1, source_target_pairs={{0,2},{2,0},{1,3},{3,1},{4,6},{6,4},{5,7},{7,5},{8,10},{10,8},{9,1... | collective-permute-start | bytes 958472 | tf_op jit(solution)/shard_map/ppermute | solution.py:199
  269.1 20.4 %collective-permute-start.23 = (bf16[4,104,384]{2,1,0:T(8,128)(2,1)S(1)}, bf16[4,104,384]{2,1,0:T(8,128)(2,1)}, u32[]{:S(2)}, u32[]{:S(2)}) collective-permute-start(bf16[4,104,384]{2,1,0:T(8,128)(2,1)S(1)} %dynamic-slice_bitcast_fusion.1), channel_id=1, source_target_pairs={{0,4},{4,0},{8,12},{12,8},{16,20},{20,16},{24,28},{28,24},{1,5},{5... | collective-permute-start | bytes 958472 | tf_op jit(solution)/shard_map/ppermute | solution.py:199
  289.1 13.7 %collective-permute-start.33 = (bf16[1,2,96,768]{3,2,1,0:T(8,128)(2,1)}, bf16[1,2,96,768]{3,2,1,0:T(8,128)(2,1)}, u32[]{:S(2)}, u32[]{:S(2)}) collective-permute-start(bf16[1,2,96,768]{3,2,1,0:T(8,128)(2,1)} %constant_dynamic-slice_fusion), channel_id=1, source_target_pairs={{0,8},{4,12},{8,0},{12,4},{16,24},{20,28},{24,16},{28,20},{1,9},{5... | collective-permute-start | bytes 884744 | tf_op jit(solution)/shard_map/ppermute | solution.py:199
  291.0 20.8 %collective-permute-start.26 = (bf16[2,2,104,384]{2,3,1,0:T(8,128)(2,1)S(1)}, bf16[2,2,104,384]{2,3,1,0:T(8,128)(2,1)S(1)}, u32[]{:S(2)}, u32[]{:S(2)}) collective-permute-start(bf16[2,2,104,384]{2,3,1,0:T(8,128)(2,1)S(1)} %fusion.43), channel_id=1, source_target_pairs={{0,16},{4,20},{8,24},{12,28},{16,0},{20,4},{24,8},{28,12},{1,17},{... | collective-permute-start | bytes 958472 | tf_op jit(solution)/shard_map/ppermute | solution.py:199
  312.0 6.1 %collective-permute-start.27 = (bf16[1,2,104,384]{2,3,1,0:T(8,128)(2,1)S(1)}, bf16[1,2,104,384]{2,3,1,0:T(8,128)(2,1)S(1)}, u32[]{:S(2)}, u32[]{:S(2)}) collective-permute-start(bf16[1,2,104,384]{2,3,1,0:T(8,128)(2,1)S(1)} %constant_dynamic-slice_fusion.1), channel_id=1, source_target_pairs={{0,8},{4,12},{8,0},{12,4},{16,24},{20,28},{24,16},{28,20},{1,9},{5... | collective-permute-start | bytes 479240 | tf_op jit(solution)/shard_map/ppermute | solution.py:199
  (46 other events, 321.7 us)
